TPU v7x, 256 devices: a whole 4x4x8 slice. The times are simulated.
256 devices in a mesh: tiles: 64 (over z, x, core), slide: 4 (over y).
Axes of the slice: x: 4, y: 4, z: 8, core: 2. Of those that a mesh axis runs over, the one named last changes fastest.
Arguments:
- activations: bfloat16 [4, 64, 64, 64, 128], P('slide', 'tiles'), may hold values from -6 to 6
- cotangent: bfloat16 [4, 64, 32, 32, 256], P('slide', 'tiles'), may hold values from -6 to 6
- weights: bfloat16 [3, 3, 128, 256], replicated, may hold values from -0.1875 to 0.1875
- tile_list: int32 [4, 64], P('slide'), may hold values from -1 to 63, as said below
Outputs:
- features_out: bfloat16 [4, 64, 32, 32, 256], P('slide', 'tiles')
- input_grad: bfloat16 [4, 64, 64, 64, 128], P('slide', 'tiles')
- weight_grad: float32 [3, 3, 128, 256], replicated
Inputs may be any that keep to these rules, and one draw needn't show every extreme that they name: `tile_list`: per slide, no grid tile is named twice; tiles that no slot names are background. In every slide each device along tiles holds at least one occupied slot, and all 1 slots of some device are occupied.
All inputs are finite; a program needn't handle non-finite values.
Results may differ from a plain program's by a relative error of at most 0.0014.
Values may be sent and summed in bfloat16 or wider, within the bound.
No kernel may reach another device: no remote copies, remote signals or barrier semaphores. Data moves between devices by JAX's collectives and lax.ppermute only.
A program may use at most 64 MiB of HBM per device.

v0:
```python
import math

import jax
import jax.numpy as jnp
from jax import lax
from jax.experimental import pallas as pl
from jax.experimental.pallas import tpu as pltpu
from jax.sharding import PartitionSpec as P


GW = 8
BF = jnp.bfloat16
F32 = jnp.float32


def grant(mebibytes):
    return pltpu.CompilerParams(vmem_limit_bytes=mebibytes << 20)


def vmem_specs(count):
    return [pl.BlockSpec(memory_space=pltpu.VMEM)] * count


def halo_matrices(listing, me, grid_rows):
    row, col = listing // GW, listing % GW
    live = listing >= 0

    def chosen(row_step, col_step):
        new_row, new_col = row + row_step, col + col_step
        inside = live & (new_row >= 0) & (new_row < grid_rows) & (new_col >= 0) & (new_col < GW)
        target = jnp.where(inside, new_row * GW + new_col, -2)
        return listing[None, :] == target[:, None]

    half = listing.shape[0] // 2
    by_row = me < half
    act = jnp.where(by_row, chosen(-1, 0), chosen(0, -1))
    cot = jnp.where(by_row, chosen(1, 0), chosen(0, 1))
    diag = chosen(-1, -1)
    below_right = chosen(1, 1)
    before = jnp.where(me == 0, diag, act & (me != half))
    return jnp.stack([before, act, cot, diag, below_right]).astype(BF)


def pack_kernel(
    act_ref, cot_ref, out_ref, row_buf, col_buf, crow_buf, ccol_buf, sems, tall, line, both
):
    copies = [
        pltpu.make_async_copy(act_ref.at[63], row_buf, sems.at[0]),
        pltpu.make_async_copy(act_ref.at[:, 56:64, :], col_buf, sems.at[1]),
        pltpu.make_async_copy(cot_ref.at[0], crow_buf, sems.at[2]),
        pltpu.make_async_copy(cot_ref.at[:, 0:8, :], ccol_buf, sems.at[3]),
    ]
    for copy in copies:
        copy.start()

    def fill(base, values, cot_values):
        line[8:72, :] = values
        line[7:8, :] = values[63:64, :]
        for slot in range(3):
            both[pl.ds(base * 8 + slot, 32, stride=8), :] = line[pl.ds(7 + slot, 32, stride=2), :]
        both[pl.ds(base * 8 + 3, 32, stride=8), :] = cot_values[:, 0:128]
        both[pl.ds(base * 8 + 4, 32, stride=8), :] = cot_values[:, 128:256]

    both[...] = jnp.zeros_like(both)
    for copy in copies:
        copy.wait()
    fill(0, row_buf[...].astype(F32), crow_buf[...].astype(F32))
    tall[...] = col_buf[...].astype(F32).reshape(512, 128)
    values = tall[pl.ds(7, 64, stride=8), :]
    tall[0:256, :] = ccol_buf[:, :, 0:128].astype(F32).reshape(256, 128)
    tall[256:512, :] = ccol_buf[:, :, 128:256].astype(F32).reshape(256, 128)
    low = tall[pl.ds(0, 32, stride=8), :]
    high = tall[pl.ds(256, 32, stride=8), :]
    fill(32, values, jnp.concatenate([low, high], axis=1))
    out_ref[...] = both[...].reshape(64, 8, 128).astype(BF)


def pack_edges(act, cot):
    return pl.pallas_call(
        pack_kernel,
        in_specs=[pl.BlockSpec(memory_space=pltpu.HBM)] * 2,
        out_specs=vmem_specs(1)[0],
        out_shape=jax.ShapeDtypeStruct((64, 8, 128), BF),
        scratch_shapes=[
            pltpu.VMEM((64, 128), BF),
            pltpu.VMEM((64, 8, 128), BF),
            pltpu.VMEM((32, 256), BF),
            pltpu.VMEM((32, 8, 256), BF),
            pltpu.SemaphoreType.DMA((4,)),
            pltpu.VMEM((512, 128), F32),
            pltpu.VMEM((72, 128), F32),
            pltpu.VMEM((512, 128), F32),
        ],
        name="pack_edges",
    )(act, cot)


def fill_patches(act_ref, even, odd, wide, left):
    def one_row(i, carry):
        for parity in range(2):
            p = 2 * i + parity
            wide[parity, 8:72, :] = act_ref[p].astype(F32)
            if left is not None:
                wide[parity, 7:8, :] = left[parity, pl.ds(i, 1), :]
        for parity in range(2):
            dest = odd if parity == 0 else even
            start = pl.multiple_of((i + parity) * 32, 32)
            for b in range(3):
                dest[pl.ds(start, 32), b * 128 : (b + 1) * 128] = wide[
                    parity, pl.ds(7 + b, 32, stride=2), :
                ].astype(BF)
        return carry

    lax.fori_loop(0, 32, one_row, 0, unroll=4)


def weight_kernel(live_ref, act_ref, cot_ref, out_ref, even, odd, wide):
    even[0:32, :] = jnp.zeros((32, 384), BF)
    for parity in range(2):
        wide[parity, 0:8, :] = jnp.zeros((8, 128), F32)
    fill_patches(act_ref, even, odd, wide, None)
    live = live_ref[0].astype(F32).astype(BF)
    cot = cot_ref[...].reshape(1024, 256) * live
    for a, rows in enumerate((even[0:1024, :], odd[...], even[32:1056, :])):
        out_ref[a * 384 : (a + 1) * 384, :] = lax.dot_general(
            rows, cot, (((0,), (0,)), ((), ())), preferred_element_type=F32
        )


def interior_weights(live, act, cot):
    return pl.pallas_call(
        weight_kernel,
        in_specs=[pl.BlockSpec(memory_space=pltpu.SMEM)] + vmem_specs(2),
        out_specs=vmem_specs(1)[0],
        out_shape=jax.ShapeDtypeStruct((1152, 256), F32),
        scratch_shapes=[
            pltpu.VMEM((1056, 384), BF),
            pltpu.VMEM((1024, 384), BF),
            pltpu.VMEM((2, 72, 128), F32),
        ],
        cost_estimate=pl.CostEstimate(
            flops=2 * 1024 * 1152 * 256, bytes_accessed=3 << 20, transcendentals=0
        ),
        compiler_params=grant(12),
        name="interior_weights",
    )(live, act, cot)


def turn_kernel(
    place_ref, pieces_ref, select_ref, grad_ref, back_ref, keep_ref, send_ref, tall
):
    tall[...] = pieces_ref[...].astype(F32).reshape(512, 128)
    slots = [tall[pl.ds(slot, 64, stride=8), :].astype(BF) for slot in range(5)]
    cot = jnp.concatenate(slots[3:5], axis=1)

    def pick(which, values):
        return jnp.dot(select_ref[which], values, preferred_element_type=F32)

    before, first, second = pick(0, slots[0]), pick(1, slots[1]), pick(1, slots[2])
    returned = pick(2, cot)
    corner = pick(4, cot)
    tall[pl.ds(0, 64, stride=8), :] = first
    tall[pl.ds(1, 64, stride=8), :] = second
    tall[pl.ds(2, 64, stride=8), :] = returned[:, 0:128]
    tall[pl.ds(3, 64, stride=8), :] = returned[:, 128:256]
    tall[pl.ds(4, 64, stride=8), :] = pick(3, slots[0])
    tall[pl.ds(5, 64, stride=8), :] = corner[:, 0:128]
    tall[pl.ds(6, 64, stride=8), :] = corner[:, 128:256]
    tall[pl.ds(7, 64, stride=8), :] = corner[:, 0:128]
    back_ref[...] = tall[...].reshape(64, 8, 128).astype(BF)
    step, core = place_ref[0], place_ref[1]

    def split(at, values):
        low, high = values[:, 0:128], values[:, 128:256]
        first_core = core == 0
        keep_ref[at, :] = jnp.where(first_core, low, high)
        send_ref[at, :] = jnp.where(first_core, high, low)

    split(pl.ds(0, 1152), grad_ref[...])
    for b, values in enumerate((before, first, second)):
        at = pl.ds(pl.multiple_of(b * step * 128, 128), 128)
        terms = lax.dot_general(
            values.astype(BF), cot, (((0,), (0,)), ((), ())), preferred_element_type=F32
        )
        split(at, grad_ref[at, :] + terms)


def turn_edges(place, pieces, select, grad):
    return pl.pallas_call(
        turn_kernel,
        in_specs=[pl.BlockSpec(memory_space=pltpu.SMEM)] + vmem_specs(3),
        out_specs=vmem_specs(3),
        out_shape=[
            jax.ShapeDtypeStruct((64, 8, 128), BF),
            jax.ShapeDtypeStruct((1152, 128), F32),
            jax.ShapeDtypeStruct((1152, 128), F32),
        ],
        scratch_shapes=[pltpu.VMEM((512, 128), F32)],
        compiler_params=grant(10),
        name="turn_edges",
    )(place, pieces, select, grad)


def sum_and_cut(place, which, parts):
    rows = parts[0].shape[0] // 4
    count = len(parts)

    def kernel(place_ref, *refs):
        own = place_ref[which]
        for hop in range(4):
            at = pl.ds(pl.multiple_of(((own + hop) & 3) * rows, rows), rows)
            total = refs[0][at, :]
            for ref in refs[1:count]:
                total = total + ref[at, :]
            refs[count + hop][...] = total

    return pl.pallas_call(
        kernel,
        in_specs=[pl.BlockSpec(memory_space=pltpu.SMEM)] + vmem_specs(count),
        out_specs=vmem_specs(4),
        out_shape=[jax.ShapeDtypeStruct((rows, 128), F32)] * 4,
        compiler_params=grant(4),
        name="sum_and_cut",
    )(place, *parts)


def sum_and_copy(parts, copies):
    count = len(parts)

    def kernel(*refs):
        total = refs[0][...]
        for ref in refs[1:count]:
            total = total + ref[...]
        for k in range(copies):
            refs[count][k] = total

    return pl.pallas_call(
        kernel,
        in_specs=vmem_specs(count),
        out_specs=vmem_specs(1)[0],
        out_shape=jax.ShapeDtypeStruct((copies,) + parts[0].shape, F32),
        compiler_params=grant(2),
    )(*parts)


def sum_scaled(parts, scale):
    def kernel(parts_ref, out_ref):
        total = parts_ref[0]
        for k in range(1, parts.shape[0]):
            total = total + parts_ref[k]
        out_ref[...] = total * scale

    return pl.pallas_call(
        kernel,
        in_specs=vmem_specs(1),
        out_specs=vmem_specs(1)[0],
        out_shape=jax.ShapeDtypeStruct(parts.shape[1:], F32),
        compiler_params=grant(2),
        name="sum_scaled",
    )(parts)


def assemble(place, which, parts):
    rows = parts[0].shape[0]

    def kernel(place_ref, *refs):
        own = place_ref[which]
        for hop in range(4):
            at = pl.ds(pl.multiple_of(((own - hop) & 3) * rows, rows), rows)
            refs[4][at, :] = refs[hop][...]

    return pl.pallas_call(
        kernel,
        in_specs=[pl.BlockSpec(memory_space=pltpu.SMEM)] + vmem_specs(4),
        out_specs=vmem_specs(1)[0],
        out_shape=jax.ShapeDtypeStruct((4 * rows, 128), F32),
        compiler_params=grant(2),
        name="assemble",
    )(place, *parts)


def final_weights(place, mine, theirs):
    rows = mine[0].shape[0]

    def kernel(place_ref, *refs):
        first_core, own = place_ref[1] == 0, place_ref[2]
        for hop in range(4):
            at = pl.ds(pl.multiple_of(((own - hop) & 3) * rows, rows), rows)
            here, there = refs[hop][...], refs[4 + hop][...]
            refs[8][at, 0:128] = jnp.where(first_core, here, there)
            refs[8][at, 128:256] = jnp.where(first_core, there, here)

    return pl.pallas_call(
        kernel,
        in_specs=[pl.BlockSpec(memory_space=pltpu.SMEM)] + vmem_specs(8),
        out_specs=vmem_specs(1)[0],
        out_shape=jax.ShapeDtypeStruct((4 * rows, 256), F32),
        compiler_params=grant(6),
        name="final_weights",
    )(place, *mine, *theirs)


def tile_kernel(
    live_ref, act_ref, cot_ref, weight_ref, halo_ref, feat_ref, grad_ref,
    even, odd, wide, tall, left, line, shift, around, mix, lines,
):
    live = live_ref[0].astype(F32)
    tall[...] = halo_ref[...].astype(F32).reshape(512, 128)
    first = tall[pl.ds(0, 32, stride=8), :]
    second = tall[pl.ds(1, 32, stride=8), :]
    line[8:40, :] = second
    line[7:8, :] = tall[4:5, :]
    even[0:32, 0:128] = line[7:39, :].astype(BF)
    even[0:32, 128:256] = first.astype(BF)
    even[0:32, 256:384] = second.astype(BF)
    left[0] = tall[pl.ds(256, 32, stride=8), :]
    left[1] = tall[pl.ds(257, 32, stride=8), :]
    fill_patches(act_ref, even, odd, wide, left)
    result = jnp.dot(even[0:1024, :], weight_ref[0:384, :], preferred_element_type=F32)
    result += jnp.dot(odd[...], weight_ref[384:768, :], preferred_element_type=F32)
    result += jnp.dot(even[32:1056, :], weight_ref[768:1152, :], preferred_element_type=F32)
    feat_ref[...] = (result * live).astype(BF).reshape(32, 32, 256)

    right = jnp.concatenate(
        [tall[pl.ds(258, 32, stride=8), :], tall[pl.ds(259, 32, stride=8), :]], axis=1
    )
    around[0:32, :] = right
    around[32:33, 0:128] = tall[5:6, :]
    around[32:33, 128:256] = tall[6:7, :]
    below = jnp.concatenate(
        [tall[pl.ds(2, 32, stride=8), :], tall[pl.ds(3, 32, stride=8), :]], axis=1
    )

    def place(i, values):
        shift[0:32, :] = values
        shift[32:33, :] = around[pl.ds(i, 1), :]
        at = pl.ds(pl.multiple_of(i * 32, 32), 32)
        mix[at, 0:256] = values.astype(BF)
        mix[at, 256:512] = shift[1:33, :].astype(BF)

    def one_row(i, carry):
        place(i, cot_ref[i].astype(F32))
        return carry

    lax.fori_loop(0, 32, one_row, 0, unroll=4)
    place(32, below)

    def tap(a, b):
        at = (3 * a + b) * 128
        return weight_ref[at : at + 128, :]

    none = jnp.zeros((128, 256), BF)

    def block(even_taps, odd_taps):
        return jnp.concatenate(
            [jnp.concatenate(even_taps, axis=1), jnp.concatenate(odd_taps, axis=1)], axis=0
        )

    def back(rows, matrix):
        return lax.dot_general(
            rows, matrix, (((1,), (1,)), ((), ())), preferred_element_type=F32
        )

    here, after = mix[0:1024, :], mix[32:1056, :]
    lines[0] = back(here, block([tap(1, 1), none], [tap(1, 2), tap(1, 0)])) * live
    lines[1] = (
        back(here, block([tap(2, 1), none], [tap(2, 2), tap(2, 0)]))
        + back(after, block([tap(0, 1), none], [tap(0, 2), tap(0, 0)]))
    ) * live

    def weave(i, carry):
        at = pl.ds(pl.multiple_of(i * 32, 32), 32)
        for parity in range(2):
            for side in range(2):
                wide[parity, pl.ds(8 + side, 32, stride=2), :] = lines[
                    parity, at, side * 128 : (side + 1) * 128
                ]
            grad_ref[2 * i + parity] = wide[parity, 8:72, :].astype(BF)
        return carry

    lax.fori_loop(0, 32, weave, 0, unroll=4)


def tile_terms(live, act, cot, weight_matrix, halo):
    return pl.pallas_call(
        tile_kernel,
        in_specs=[pl.BlockSpec(memory_space=pltpu.SMEM)] + vmem_specs(4),
        out_specs=vmem_specs(2),
        out_shape=[
            jax.ShapeDtypeStruct((32, 32, 256), BF),
            jax.ShapeDtypeStruct((64, 64, 128), BF),
        ],
        scratch_shapes=[
            pltpu.VMEM((1056, 384), BF),
            pltpu.VMEM((1024, 384), BF),
            pltpu.VMEM((2, 72, 128), F32),
            pltpu.VMEM((512, 128), F32),
            pltpu.VMEM((2, 32, 128), F32),
            pltpu.VMEM((40, 128), F32),
            pltpu.VMEM((40, 256), F32),
            pltpu.VMEM((40, 256), F32),
            pltpu.VMEM((1056, 512), BF),
            pltpu.VMEM((2, 1024, 256), F32),
        ],
        cost_estimate=pl.CostEstimate(
            flops=5 * 1024 * 1152 * 256, bytes_accessed=4 << 20, transcendentals=0
        ),
        compiler_params=grant(24),
        name="tile_terms",
    )(live, act, cot, weight_matrix, halo)


def shards(activations, cotangent, weights, tile_list):
    act, cot = activations[0, 0], cotangent[0, 0]
    slots = lax.axis_size("tiles")
    slides = lax.axis_size("slide")
    half_side = cot.shape[0]
    listing = tile_list[0]
    me = lax.axis_index("tiles")
    live = (lax.dynamic_slice_in_dim(listing, me, 1) >= 0).astype(jnp.int32)
    own = lax.axis_index("slide")
    step = jnp.where(me < slots // 2, 1, 3)
    place = jnp.stack([step, me & 1, own, (me >> 1) & 3]).astype(jnp.int32)
    select = halo_matrices(listing, me, slots // GW)
    weight_matrix = weights.reshape(-1, weights.shape[3])

    partner = [(t, t ^ 1) for t in range(slots)]
    columns = [[z * 8 + rest for z in range(8)] for rest in range(8)]

    def over_slide(values, hop):
        return lax.ppermute(values, "slide", [(i, (i + hop) % slides) for i in range(slides)])

    def over_x(values, hop):
        pairs = [(t, (t & ~6) | ((((t >> 1) + hop) & 3) << 1)) for t in range(slots)]
        return lax.ppermute(values, "tiles", pairs)

    pieces = lax.all_to_all(pack_edges(act, cot), "tiles", 0, 0, tiled=True)
    inner = interior_weights(live, act, cot)
    back, keep, send = turn_edges(place, pieces, select, inner)

    got = lax.ppermute(send, "tiles", partner)
    quarters = sum_and_cut(place, 2, [keep, got])
    moved = []
    for hop in range(1, 4):
        moved.append(over_slide(quarters[hop], hop))
    halo = lax.all_to_all(back, "tiles", 0, 0, tiled=True)
    cuts = sum_and_cut(place, 3, [quarters[0]] + moved)
    moved = []
    for hop in range(1, 4):
        moved.append(over_x(cuts[hop], hop))
    copies = sum_and_copy([cuts[0]] + moved, 8)
    copies, halo = lax.optimization_barrier((copies, halo))
    parts = lax.all_to_all(copies, "tiles", 0, 0, tiled=True, axis_index_groups=columns)
    grad_scale = 1.0 / math.sqrt(slides * slots * half_side * half_side)
    eighth = sum_scaled(parts, grad_scale)

    features_out, input_grad = tile_terms(live, act, cot, weight_matrix, halo)

    quarter = assemble(place, 3, [eighth] + [over_x(eighth, hop) for hop in range(1, 4)])
    mine = [quarter]
    for hop in range(1, 4):
        mine.append(over_slide(quarter, hop))
    theirs = []
    for hop in range(4):
        theirs.append(lax.ppermute(mine[hop], "tiles", partner))
    weight_grad = final_weights(place, mine, theirs).reshape(weights.shape)
    return (features_out[None, None], input_grad[None, None], weight_grad)


def solution(mesh):
    placed = (
        P("slide", "tiles", None, None, None),
        P("slide", "tiles", None, None, None),
        P(),
        P("slide", None),
    )
    return jax.shard_map(
        shards,
        mesh=mesh,
        in_specs=placed,
        out_specs=(
            P("slide", "tiles", None, None, None),
            P("slide", "tiles", None, None, None),
            P(),
        ),
        check_vma=False,
    )
```

profile of v0, /device:TPU:1, one launch (start us, length us, event | category | flops | bytes accessed | tf_op | source)
XLA Modules:
  0.0 100.9 jit_solution(6058623560030105726)
XLA Ops:
  0.7 1.9 %pack_edges.1 = bf16[64,8,128]{2,1,0:T(8,128)(2,1)} custom-call(bf16[64,64,128]{2,1,0:T(8,128)(2,1)} %bitcast.35, bf16[32,32,256]{2,1,0:T(8,128)(2,1)} %bitcast.38), custom_call_target="tpu_custom_call" | custom-call | tf_op jit(solution)/shard_map/pack_edges/pallas_call | solution.py:79
  2.6 13.0 %all-to-all-start = ((bf16[64,8,128]{2,1,0:T(8,128)(2,1)}), bf16[64,8,128]{2,1,0:T(8,128)(2,1)S(1)}, u32[]{:S(2)}, u32[]{:S(2)}) async-start(bf16[64,8,128]{2,1,0:T(8,128)(2,1)} %pack_edges.1), calls=%async_computation | async-start | bytes 262144 | tf_op jit(solution)/shard_map/all_to_all | solution.py:437
  15.6 0.1 fusion
  15.7 0.1 fusion.1
  15.8 0.1 select_dynamic-update-slice_fusion
  15.9 0.1 compare_dynamic-update-slice_fusion
  16.0 0.1 compare_dynamic-update-slice_fusion.1
  16.1 0.6 fusion.2
  17.4 1.3 %interior_weights.1.grad_ref = f32[1152,256]{1,0:T(8,128)S(1)} custom-call(s32[1]{0:T(128)} %bitcast.live_ref, bf16[64,64,128]{2,1,0:T(8,128)(2,1)S(1)} %bitcast.36, bf16[32,32,256]{2,1,0:T(8,128)(2,1)S(1)} %bitcast.39), custom_call_target="tpu_custom_call" | custom-call | flops 603979776 | bytes 3145728 | tf_op jit(solution)/shard_map/interior_weights/pallas_call | solution.py:131
  18.7 0.6 pad_add_fusion.place_ref
  19.2 7.4 %all-to-all-done.pieces_ref = bf16[64,8,128]{2,1,0:T(8,128)(2,1)S(1)} async-done(((bf16[64,8,128]{2,1,0:T(8,128)(2,1)}), bf16[64,8,128]{2,1,0:T(8,128)(2,1)S(1)}, u32[]{:S(2)}, u32[]{:S(2)}) %all-to-all-start) | async-done | bytes 131104 | tf_op jit(solution)/shard_map/all_to_all | solution.py:437
  26.7 0.6 copy-done.3
  27.2 1.8 %turn_edges.1 = (bf16[64,8,128]{2,1,0:T(8,128)(2,1)S(1)}, f32[1152,128]{1,0:T(8,128)S(1)}, f32[1152,128]{1,0:T(8,128)}) custom-call(s32[4]{0:T(128)S(1)} %copy-done.3, bf16[64,8,128]{2,1,0:T(8,128)(2,1)S(1)} %all-to-all-done.pieces_ref, bf16[5,64,64]{2,1,0:T(8,128)(2,1)S(1)} %convert_element_type.10.select_ref, f32[1152,256]{1,0:T(8,128)S(1)} %interior_weights.1.grad_ref), custom_call_target="tpu_custom_call" | custom-call | tf_op jit(solution)/shard_map/turn_edges/pallas_call | solution.py:189
  29.0 0.7 copy-done.2
  29.7 0.4 collective-permute-start
  30.1 4.2 %all-to-all-start.1 = ((bf16[64,8,128]{2,1,0:T(8,128)(2,1)}), bf16[64,8,128]{2,1,0:T(8,128)(2,1)S(1)}, u32[]{:S(2)}, u32[]{:S(2)}) async-start(bf16[64,8,128]{2,1,0:T(8,128)(2,1)} %copy-done.2), calls=%async_computation.1 | async-start | bytes 262144 | tf_op jit(solution)/shard_map/all_to_all | solution.py:446
  34.3 0.0 collective-permute-done.refs_1_
  34.3 0.6 copy-done.4
  34.9 0.6 sum_and_cut.2
  35.5 0.0 copy-start.6
  35.5 1.4 %collective-permute-start.1 = (f32[288,128]{1,0:T(8,128)S(1)}, f32[288,128]{1,0:T(8,128)S(1)}, u32[]{:S(2)}, u32[]{:S(2)}) collective-permute-start(f32[288,128]{1,0:T(8,128)S(1)} %get-tuple-element.21), channel_id=1, source_target_pairs={{0,1},{1,2},{2,3},{3,0},{4,5},{5,6},{6,7},{7,4},{8,9},{9,10},{10,1... | collective-permute-start | bytes 442376 | tf_op jit(solution)/shard_map/ppermute | solution.py:431
  36.9 2.6 %collective-permute-start.2 = (f32[288,128]{1,0:T(8,128)S(1)}, f32[288,128]{1,0:T(8,128)S(1)}, u32[]{:S(2)}, u32[]{:S(2)}) collective-permute-start(f32[288,128]{1,0:T(8,128)S(1)} %get-tuple-element.22), channel_id=1, source_target_pairs={{0,2},{1,3},{2,0},{3,1},{4,6},{5,7},{6,4},{7,5},{8,10},{9,11},{10,... | collective-permute-start | bytes 442376 | tf_op jit(solution)/shard_map/ppermute | solution.py:431
  39.5 1.1 %collective-permute-start.3 = (f32[288,128]{1,0:T(8,128)S(1)}, f32[288,128]{1,0:T(8,128)S(1)}, u32[]{:S(2)}, u32[]{:S(2)}) collective-permute-start(f32[288,128]{1,0:T(8,128)S(1)} %get-tuple-element.23), channel_id=1, source_target_pairs={{0,3},{1,0},{2,1},{3,2},{4,7},{5,4},{6,5},{7,6},{8,11},{9,8},{10,9... | collective-permute-start | bytes 442376 | tf_op jit(solution)/shard_map/ppermute | solution.py:431
  40.6 1.2 %collective-permute-done.1.refs_1_ = f32[288,128]{1,0:T(8,128)S(1)} collective-permute-done((f32[288,128]{1,0:T(8,128)S(1)}, f32[288,128]{1,0:T(8,128)S(1)}, u32[]{:S(2)}, u32[]{:S(2)}) %collective-permute-start.1) | collective-permute-done | bytes 147488 | tf_op jit(solution)/shard_map/ppermute | solution.py:431
  41.8 4.3 %collective-permute-done.2.refs_2_ = f32[288,128]{1,0:T(8,128)S(1)} collective-permute-done((f32[288,128]{1,0:T(8,128)S(1)}, f32[288,128]{1,0:T(8,128)S(1)}, u32[]{:S(2)}, u32[]{:S(2)}) %collective-permute-start.2) | collective-permute-done | bytes 147488 | tf_op jit(solution)/shard_map/ppermute | solution.py:431
  46.0 0.0 collective-permute-done.3.refs_3_
  46.1 0.6 sum_and_cut.3
  46.6 1.6 %collective-permute-start.4 = (f32[72,128]{1,0:T(8,128)S(1)}, f32[72,128]{1,0:T(8,128)S(1)}, u32[]{:S(2)}, u32[]{:S(2)}) collective-permute-start(f32[72,128]{1,0:T(8,128)S(1)} %get-tuple-element.25), channel_id=1, source_target_pairs={{0,8},{4,12},{8,16},{12,20},{16,24},{20,28},{24,0},{28,4},{32,40},... | collective-permute-start | bytes 110600 | tf_op jit(solution)/shard_map/ppermute | solution.py:435
  48.2 2.4 %collective-permute-start.5 = (f32[72,128]{1,0:T(8,128)S(1)}, f32[72,128]{1,0:T(8,128)S(1)}, u32[]{:S(2)}, u32[]{:S(2)}) collective-permute-start(f32[72,128]{1,0:T(8,128)S(1)} %get-tuple-element.26), channel_id=1, source_target_pairs={{0,16},{4,20},{8,24},{12,28},{16,0},{20,4},{24,8},{28,12},{32,48},... | collective-permute-start | bytes 110600 | tf_op jit(solution)/shard_map/ppermute | solution.py:435
  50.6 1.2 %collective-permute-start.6 = (f32[72,128]{1,0:T(8,128)S(1)}, f32[72,128]{1,0:T(8,128)S(1)}, u32[]{:S(2)}, u32[]{:S(2)}) collective-permute-start(f32[72,128]{1,0:T(8,128)S(1)} %get-tuple-element.27), channel_id=1, source_target_pairs={{0,24},{4,28},{8,0},{12,4},{16,8},{20,12},{24,16},{28,20},{32,56},... | collective-permute-start | bytes 110600 | tf_op jit(solution)/shard_map/ppermute | solution.py:435
  51.8 0.8 collective-permute-done.5.refs_2_
  52.6 1.6 %collective-permute-done.6.refs_3_ = f32[72,128]{1,0:T(8,128)S(1)} collective-permute-done((f32[72,128]{1,0:T(8,128)S(1)}, f32[72,128]{1,0:T(8,128)S(1)}, u32[]{:S(2)}, u32[]{:S(2)}) %collective-permute-start.6) | collective-permute-done | bytes 36896 | tf_op jit(solution)/shard_map/ppermute | solution.py:435
  54.2 15.9 %all_to_all.15.parts_ref = f32[8,72,128]{2,1,0:T(8,128)S(1)} all-to-all(f32[8,72,128]{2,1,0:T(8,128)S(1)} %shard_map.67), channel_id=1, replica_groups={{0,32,64,96,128,160,192,224},{4,36,68,100,132,164,196,228},{8,40,72,104..., dimensions={0} | all-to-all | bytes 589824 | tf_op jit(solution)/shard_map/all_to_all | solution.py:453
  70.1 2.4 %collective-permute-start.9 = (f32[72,128]{1,0:T(8,128)S(1)}, f32[72,128]{1,0:T(8,128)S(1)}, u32[]{:S(2)}, u32[]{:S(2)}) collective-permute-start(f32[72,128]{1,0:T(8,128)S(1)} %sum_scaled.1.refs_0_), channel_id=1, source_target_pairs={{0,24},{4,28},{8,0},{12,4},{16,8},{20,12},{24,16},{28,20},{32,56},... | collective-permute-start | bytes 110600 | tf_op jit(solution)/shard_map/ppermute | solution.py:435
  72.6 0.7 collective-permute-start.7
  73.2 0.4 collective-permute-done.9.refs_3_
  73.6 3.3 %collective-permute-done.8.refs_2_ = f32[72,128]{1,0:T(8,128)S(1)} collective-permute-done((f32[72,128]{1,0:T(8,128)S(1)}, f32[72,128]{1,0:T(8,128)S(1)}, u32[]{:S(2)}, u32[]{:S(2)}) %collective-permute-start.8) | collective-permute-done | bytes 36896 | tf_op jit(solution)/shard_map/ppermute | solution.py:435
  77.0 0.0 collective-permute-done.7.refs_1_
  77.0 0.6 assemble.1.refs_0_
  77.5 2.2 %collective-permute-start.12 = (f32[288,128]{1,0:T(8,128)S(1)}, f32[288,128]{1,0:T(8,128)S(1)}, u32[]{:S(2)}, u32[]{:S(2)}) collective-permute-start(f32[288,128]{1,0:T(8,128)S(1)} %assemble.1.refs_0_), channel_id=1, source_target_pairs={{0,3},{1,0},{2,1},{3,2},{4,7},{5,4},{6,5},{7,6},{8,11},{9,8},{10,9... | collective-permute-start | bytes 442376 | tf_op jit(solution)/shard_map/ppermute | solution.py:431
  79.7 0.9 collective-permute-start.11
  80.6 0.0 collective-permute-start.10
  80.6 6.3 %collective-permute-start.13 = (f32[288,128]{1,0:T(8,128)S(1)}, f32[288,128]{1,0:T(8,128)S(1)}, u32[]{:S(2)}, u32[]{:S(2)}) collective-permute-start(f32[288,128]{1,0:T(8,128)S(1)} %assemble.1.refs_0_), channel_id=1, source_target_pairs={{0,4},{4,0},{8,12},{12,8},{16,20},{20,16},{24,28},{28,24},{32,36},... | collective-permute-start | bytes 442376 | tf_op jit(solution)/shard_map/ppermute | solution.py:465
  86.9 2.6 %collective-permute-start.16 = (f32[288,128]{1,0:T(8,128)S(1)}, f32[288,128]{1,0:T(8,128)S(1)}, u32[]{:S(2)}, u32[]{:S(2)}) collective-permute-start(f32[288,128]{1,0:T(8,128)S(1)} %collective-permute-done.12.refs_3_), channel_id=1, source_target_pairs={{0,4},{4,0},{8,12},{12,8},{16,20},{20,16},{24,28},{28,24},{32,36},... | collective-permute-start | bytes 442376 | tf_op jit(solution)/shard_map/ppermute | solution.py:465
  89.5 2.5 %collective-permute-start.15 = (f32[288,128]{1,0:T(8,128)S(1)}, f32[288,128]{1,0:T(8,128)S(1)}, u32[]{:S(2)}, u32[]{:S(2)}) collective-permute-start(f32[288,128]{1,0:T(8,128)S(1)} %collective-permute-done.11.refs_2_), channel_id=1, source_target_pairs={{0,4},{4,0},{8,12},{12,8},{16,20},{20,16},{24,28},{28,24},{32,36},... | collective-permute-start | bytes 442376 | tf_op jit(solution)/shard_map/ppermute | solution.py:465
  92.0 1.5 %collective-permute-start.14 = (f32[288,128]{1,0:T(8,128)S(1)}, f32[288,128]{1,0:T(8,128)S(1)}, u32[]{:S(2)}, u32[]{:S(2)}) collective-permute-start(f32[288,128]{1,0:T(8,128)S(1)} %collective-permute-done.10.refs_1_), channel_id=1, source_target_pairs={{0,4},{4,0},{8,12},{12,8},{16,20},{20,16},{24,28},{28,24},{32,36},... | collective-permute-start | bytes 442376 | tf_op jit(solution)/shard_map/ppermute | solution.py:465
  93.5 5.8 %tile_terms.1 = (bf16[32,32,256]{2,1,0:T(8,128)(2,1)}, bf16[64,64,128]{2,1,0:T(8,128)(2,1)}) custom-call(s32[1]{0:T(128)} %bitcast.live_ref, bf16[64,64,128]{2,1,0:T(8,128)(2,1)S(1)} %bitcast.37, bf16[32,32,256]{2,1,0:T(8,128)(2,1)S(1)} %bitcast.40, bf16[1152,256]{1,0:T(8,128)(2,1)S(1)} %bitcast.41, bf16[64,8,128]{2,1,0:T(8,128)(2,1)S(1)} %all-to-all-done.1.halo_ref), custom_call_target="tpu_custom_call" | custom-call | flops 1509949440 | bytes 4194304 | tf_op jit(solution)/shard_map/tile_terms/pallas_call | solution.py:385
  99.3 1.6 %final_weights.1 = f32[1152,256]{1,0:T(8,128)} custom-call(s32[4]{0:T(128)S(1)} %copy-done.5, f32[288,128]{1,0:T(8,128)S(1)} %assemble.1.refs_0_, f32[288,128]{1,0:T(8,128)S(1)} %collective-permute-done.10.refs_1_, f32[288,128]{1,0:T(8,128)S(1)} %collective-permute-done.11.refs_2_, f32[288,128]{1,0:T(8,128)S(1)} %collective-permute-done.12.refs_3_, ...), custom_call_target="tpu_custom_call" | custom-call | tf_op jit(solution)/shard_map/final_weights/pallas_call | solution.py:293
  (27 shorter events, 0.1 us)
Async XLA Ops:
  0.6 16.8 %copy-start.1 = (bf16[1,1,32,32,256]{4,3,2,1,0:T(8,128)(2,1)S(1)}, bf16[1,1,32,32,256]{4,3,2,1,0:T(8,128)(2,1)}, u32[]{:S(2)}) copy-start(bf16[1,1,32,32,256]{4,3,2,1,0:T(8,128)(2,1)} %param.5) | copy-start | bytes 1572868
  0.6 16.8 %copy-start = (bf16[1,1,64,64,128]{4,3,2,1,0:T(8,128)(2,1)S(1)}, bf16[1,1,64,64,128]{4,3,2,1,0:T(8,128)(2,1)}, u32[]{:S(2)}) copy-start(bf16[1,1,64,64,128]{4,3,2,1,0:T(8,128)(2,1)} %param.4) | copy-start | bytes 3145732
  0.7 14.9 %copy-start.7 = (s32[1,64]{1,0:T(1,128)S(1)}, s32[1,64]{1,0:T(1,128)}, u32[]{:S(2)}) copy-start(s32[1,64]{1,0:T(1,128)} %param.7) | copy-start | bytes 772
  2.6 24.1 %all-to-all-start = ((bf16[64,8,128]{2,1,0:T(8,128)(2,1)}), bf16[64,8,128]{2,1,0:T(8,128)(2,1)S(1)}, u32[]{:S(2)}, u32[]{:S(2)}) async-start(bf16[64,8,128]{2,1,0:T(8,128)(2,1)} %pack_edges.1), calls=%async_computation | async-start | bytes 262144 | tf_op jit(solution)/shard_map/all_to_all | solution.py:437
  26.7 0.6 copy-start.3
  29.0 0.7 copy-start.2
  29.7 16.4 %copy-start.5 = (s32[4]{0:T(128)S(1)}, s32[4]{0:T(128)}, u32[]{:S(2)}) copy-start(s32[4]{0:T(128)} %pad_add_fusion.place_ref) | copy-start | bytes 52
  29.7 4.6 %collective-permute-start = (f32[1152,128]{1,0:T(8,128)}, f32[1152,128]{1,0:T(8,128)S(1)}, u32[]{:S(2)}, u32[]{:S(2)}) collective-permute-start(f32[1152,128]{1,0:T(8,128)} %get-tuple-element.19), channel_id=1, source_target_pairs={{0,4},{4,0},{8,12},{12,8},{16,20},{20,16},{24,28},{28,24},{32,36},... | collective-permute-start | bytes 1769480 | tf_op jit(solution)/shard_map/ppermute | solution.py:441
  30.1 24.1 %all-to-all-start.1 = ((bf16[64,8,128]{2,1,0:T(8,128)(2,1)}), bf16[64,8,128]{2,1,0:T(8,128)(2,1)S(1)}, u32[]{:S(2)}, u32[]{:S(2)}) async-start(bf16[64,8,128]{2,1,0:T(8,128)(2,1)} %copy-done.2), calls=%async_computation.1 | async-start | bytes 262144 | tf_op jit(solution)/shard_map/all_to_all | solution.py:446
  34.3 0.6 copy-start.4
  35.5 58.0 %copy-start.6 = (bf16[3,3,128,256]{3,2,1,0:T(8,128)(2,1)S(1)}, bf16[3,3,128,256]{3,2,1,0:T(8,128)(2,1)}, u32[]{:S(2)}) copy-start(bf16[3,3,128,256]{3,2,1,0:T(8,128)(2,1)} %param.6) | copy-start | bytes 1769476
  35.5 6.3 %collective-permute-start.1 = (f32[288,128]{1,0:T(8,128)S(1)}, f32[288,128]{1,0:T(8,128)S(1)}, u32[]{:S(2)}, u32[]{:S(2)}) collective-permute-start(f32[288,128]{1,0:T(8,128)S(1)} %get-tuple-element.21), channel_id=1, source_target_pairs={{0,1},{1,2},{2,3},{3,0},{4,5},{5,6},{6,7},{7,4},{8,9},{9,10},{10,1... | collective-permute-start | bytes 442376 | tf_op jit(solution)/shard_map/ppermute | solution.py:431
  36.9 9.2 %collective-permute-start.2 = (f32[288,128]{1,0:T(8,128)S(1)}, f32[288,128]{1,0:T(8,128)S(1)}, u32[]{:S(2)}, u32[]{:S(2)}) collective-permute-start(f32[288,128]{1,0:T(8,128)S(1)} %get-tuple-element.22), channel_id=1, source_target_pairs={{0,2},{1,3},{2,0},{3,1},{4,6},{5,7},{6,4},{7,5},{8,10},{9,11},{10,... | collective-permute-start | bytes 442376 | tf_op jit(solution)/shard_map/ppermute | solution.py:431
  39.5 6.6 %collective-permute-start.3 = (f32[288,128]{1,0:T(8,128)S(1)}, f32[288,128]{1,0:T(8,128)S(1)}, u32[]{:S(2)}, u32[]{:S(2)}) collective-permute-start(f32[288,128]{1,0:T(8,128)S(1)} %get-tuple-element.23), channel_id=1, source_target_pairs={{0,3},{1,0},{2,1},{3,2},{4,7},{5,4},{6,5},{7,6},{8,11},{9,8},{10,9... | collective-permute-start | bytes 442376 | tf_op jit(solution)/shard_map/ppermute | solution.py:431
  46.6 5.2 %collective-permute-start.4 = (f32[72,128]{1,0:T(8,128)S(1)}, f32[72,128]{1,0:T(8,128)S(1)}, u32[]{:S(2)}, u32[]{:S(2)}) collective-permute-start(f32[72,128]{1,0:T(8,128)S(1)} %get-tuple-element.25), channel_id=1, source_target_pairs={{0,8},{4,12},{8,16},{12,20},{16,24},{20,28},{24,0},{28,4},{32,40},... | collective-permute-start | bytes 110600 | tf_op jit(solution)/shard_map/ppermute | solution.py:435
  48.2 4.3 %collective-permute-start.5 = (f32[72,128]{1,0:T(8,128)S(1)}, f32[72,128]{1,0:T(8,128)S(1)}, u32[]{:S(2)}, u32[]{:S(2)}) collective-permute-start(f32[72,128]{1,0:T(8,128)S(1)} %get-tuple-element.26), channel_id=1, source_target_pairs={{0,16},{4,20},{8,24},{12,28},{16,0},{20,4},{24,8},{28,12},{32,48},... | collective-permute-start | bytes 110600 | tf_op jit(solution)/shard_map/ppermute | solution.py:435
  50.6 3.5 %collective-permute-start.6 = (f32[72,128]{1,0:T(8,128)S(1)}, f32[72,128]{1,0:T(8,128)S(1)}, u32[]{:S(2)}, u32[]{:S(2)}) collective-permute-start(f32[72,128]{1,0:T(8,128)S(1)} %get-tuple-element.27), channel_id=1, source_target_pairs={{0,24},{4,28},{8,0},{12,4},{16,8},{20,12},{24,16},{28,20},{32,56},... | collective-permute-start | bytes 110600 | tf_op jit(solution)/shard_map/ppermute | solution.py:435
  70.1 3.5 %collective-permute-start.9 = (f32[72,128]{1,0:T(8,128)S(1)}, f32[72,128]{1,0:T(8,128)S(1)}, u32[]{:S(2)}, u32[]{:S(2)}) collective-permute-start(f32[72,128]{1,0:T(8,128)S(1)} %sum_scaled.1.refs_0_), channel_id=1, source_target_pairs={{0,24},{4,28},{8,0},{12,4},{16,8},{20,12},{24,16},{28,20},{32,56},... | collective-permute-start | bytes 110600 | tf_op jit(solution)/shard_map/ppermute | solution.py:435
  72.6 4.4 %collective-permute-start.8 = (f32[72,128]{1,0:T(8,128)S(1)}, f32[72,128]{1,0:T(8,128)S(1)}, u32[]{:S(2)}, u32[]{:S(2)}) collective-permute-start(f32[72,128]{1,0:T(8,128)S(1)} %sum_scaled.1.refs_0_), channel_id=1, source_target_pairs={{0,16},{4,20},{8,24},{12,28},{16,0},{20,4},{24,8},{28,12},{32,48},... | collective-permute-start | bytes 110600 | tf_op jit(solution)/shard_map/ppermute | solution.py:435
  72.6 4.4 %collective-permute-start.7 = (f32[72,128]{1,0:T(8,128)S(1)}, f32[72,128]{1,0:T(8,128)S(1)}, u32[]{:S(2)}, u32[]{:S(2)}) collective-permute-start(f32[72,128]{1,0:T(8,128)S(1)} %sum_scaled.1.refs_0_), channel_id=1, source_target_pairs={{0,8},{4,12},{8,16},{12,20},{16,24},{20,28},{24,0},{28,4},{32,40},... | collective-permute-start | bytes 110600 | tf_op jit(solution)/shard_map/ppermute | solution.py:435
  77.5 9.4 %collective-permute-start.12 = (f32[288,128]{1,0:T(8,128)S(1)}, f32[288,128]{1,0:T(8,128)S(1)}, u32[]{:S(2)}, u32[]{:S(2)}) collective-permute-start(f32[288,128]{1,0:T(8,128)S(1)} %assemble.1.refs_0_), channel_id=1, source_target_pairs={{0,3},{1,0},{2,1},{3,2},{4,7},{5,4},{6,5},{7,6},{8,11},{9,8},{10,9... | collective-permute-start | bytes 442376 | tf_op jit(solution)/shard_map/ppermute | solution.py:431
  79.7 9.8 %collective-permute-start.11 = (f32[288,128]{1,0:T(8,128)S(1)}, f32[288,128]{1,0:T(8,128)S(1)}, u32[]{:S(2)}, u32[]{:S(2)}) collective-permute-start(f32[288,128]{1,0:T(8,128)S(1)} %assemble.1.refs_0_), channel_id=1, source_target_pairs={{0,2},{1,3},{2,0},{3,1},{4,6},{5,7},{6,4},{7,5},{8,10},{9,11},{10,... | collective-permute-start | bytes 442376 | tf_op jit(solution)/shard_map/ppermute | solution.py:431
  80.6 11.4 %collective-permute-start.10 = (f32[288,128]{1,0:T(8,128)S(1)}, f32[288,128]{1,0:T(8,128)S(1)}, u32[]{:S(2)}, u32[]{:S(2)}) collective-permute-start(f32[288,128]{1,0:T(8,128)S(1)} %assemble.1.refs_0_), channel_id=1, source_target_pairs={{0,1},{1,2},{2,3},{3,0},{4,5},{5,6},{6,7},{7,4},{8,9},{9,10},{10,1... | collective-permute-start | bytes 442376 | tf_op jit(solution)/shard_map/ppermute | solution.py:431
  80.6 18.6 %collective-permute-start.13 = (f32[288,128]{1,0:T(8,128)S(1)}, f32[288,128]{1,0:T(8,128)S(1)}, u32[]{:S(2)}, u32[]{:S(2)}) collective-permute-start(f32[288,128]{1,0:T(8,128)S(1)} %assemble.1.refs_0_), channel_id=1, source_target_pairs={{0,4},{4,0},{8,12},{12,8},{16,20},{20,16},{24,28},{28,24},{32,36},... | collective-permute-start | bytes 442376 | tf_op jit(solution)/shard_map/ppermute | solution.py:465
  86.9 12.4 %collective-permute-start.16 = (f32[288,128]{1,0:T(8,128)S(1)}, f32[288,128]{1,0:T(8,128)S(1)}, u32[]{:S(2)}, u32[]{:S(2)}) collective-permute-start(f32[288,128]{1,0:T(8,128)S(1)} %collective-permute-done.12.refs_3_), channel_id=1, source_target_pairs={{0,4},{4,0},{8,12},{12,8},{16,20},{20,16},{24,28},{28,24},{32,36},... | collective-permute-start | bytes 442376 | tf_op jit(solution)/shard_map/ppermute | solution.py:465
  89.5 9.7 %collective-permute-start.15 = (f32[288,128]{1,0:T(8,128)S(1)}, f32[288,128]{1,0:T(8,128)S(1)}, u32[]{:S(2)}, u32[]{:S(2)}) collective-permute-start(f32[288,128]{1,0:T(8,128)S(1)} %collective-permute-done.11.refs_2_), channel_id=1, source_target_pairs={{0,4},{4,0},{8,12},{12,8},{16,20},{20,16},{24,28},{28,24},{32,36},... | collective-permute-start | bytes 442376 | tf_op jit(solution)/shard_map/ppermute | solution.py:465
  92.0 7.3 %collective-permute-start.14 = (f32[288,128]{1,0:T(8,128)S(1)}, f32[288,128]{1,0:T(8,128)S(1)}, u32[]{:S(2)}, u32[]{:S(2)}) collective-permute-start(f32[288,128]{1,0:T(8,128)S(1)} %collective-permute-done.10.refs_1_), channel_id=1, source_target_pairs={{0,4},{4,0},{8,12},{12,8},{16,20},{20,16},{24,28},{28,24},{32,36},... | collective-permute-start | bytes 442376 | tf_op jit(solution)/shard_map/ppermute | solution.py:465
where the time goes:
time: 101 us
  starting transfers between devices  46.8 us (46%)
  waiting for transfers between devices  19 us (19%)
  blocking collectives  15.9 us (16%)
  Pallas kernels  14.1 us (14%)
  local copies, waits for them, and re-layouts  1.86 us (2%)
  other arithmetic  1.68 us (2%)
  between operations  1.52 us (2%)
    all_to_all x1, blocking collectives, shards(): lax.all_to_all(copies, 'tiles', 0, 0, tiled=True, axis_index_groups=columns)  15.9 us
    all_to_all x1, starting transfers between devices, shards(): pieces = lax.all_to_all(pack_edges(act, cot), 'tiles', 0, 0, tiled=True)  13 us
    ppermute x4, starting transfers between devices, shards(): theirs.append(lax.ppermute(mine[hop], 'tiles', partner))  12.8 us
    ppermute x6, starting transfers between devices, over_x(): return lax.ppermute(values, 'tiles', pairs)  8.29 us
    ppermute x6, starting transfers between devices, over_slide(): lax.ppermute(values, 'slide', [(i, (i + hop) % slides) for i in range(sli...  8.15 us
    all_to_all x1, waiting for transfers between devices, shards(): pieces = lax.all_to_all(pack_edges(act, cot), 'tiles', 0, 0, tiled=True)  7.41 us
    ppermute x6, waiting for transfers between devices, over_x(): return lax.ppermute(values, 'tiles', pairs)  6.06 us
    pallas_call x1, Pallas kernels, tile_terms(): pl.pallas_call(tile_kernel, in_specs=[pl.BlockSpec(memory_space=pltpu.SME...  5.78 us
  transfers between devices with their start and end apart: 19, of which 7 were waited for; matrix products, arithmetic and copies ran while one was open for 2% of the time, Pallas kernels for 8%

commit v1 on v0

--- a/solution.py
+++ b/solution.py
@@ -114,25 +114,29 @@
     lax.fori_loop(0, 32, one_row, 0, unroll=4)
 
 
-def weight_kernel(live_ref, act_ref, cot_ref, out_ref, even, odd, wide):
+def weight_kernel(place_ref, act_ref, cot_ref, keep_ref, send_ref, even, odd, wide):
     even[0:32, :] = jnp.zeros((32, 384), BF)
     for parity in range(2):
         wide[parity, 0:8, :] = jnp.zeros((8, 128), F32)
     fill_patches(act_ref, even, odd, wide, None)
-    live = live_ref[0].astype(F32).astype(BF)
+    live = place_ref[4].astype(F32).astype(BF)
+    first_core = place_ref[1] == 0
     cot = cot_ref[...].reshape(1024, 256) * live
     for a, rows in enumerate((even[0:1024, :], odd[...], even[32:1056, :])):
-        out_ref[a * 384 : (a + 1) * 384, :] = lax.dot_general(
+        terms = lax.dot_general(
             rows, cot, (((0,), (0,)), ((), ())), preferred_element_type=F32
         )
-
-
-def interior_weights(live, act, cot):
+        at = slice(a * 384, (a + 1) * 384)
+        keep_ref[at, :] = jnp.where(first_core, terms[:, 0:128], terms[:, 128:256])
+        send_ref[at, :] = jnp.where(first_core, terms[:, 128:256], terms[:, 0:128])
+
+
+def interior_weights(place, act, cot):
     return pl.pallas_call(
         weight_kernel,
         in_specs=[pl.BlockSpec(memory_space=pltpu.SMEM)] + vmem_specs(2),
-        out_specs=vmem_specs(1)[0],
-        out_shape=jax.ShapeDtypeStruct((1152, 256), F32),
+        out_specs=vmem_specs(2),
+        out_shape=[jax.ShapeDtypeStruct((1152, 128), F32)] * 2,
         scratch_shapes=[
             pltpu.VMEM((1056, 384), BF),
             pltpu.VMEM((1024, 384), BF),
@@ -143,11 +147,11 @@
         ),
         compiler_params=grant(12),
         name="interior_weights",
-    )(live, act, cot)
+    )(place, act, cot)
 
 
 def turn_kernel(
-    place_ref, pieces_ref, select_ref, grad_ref, back_ref, keep_ref, send_ref, tall
+    place_ref, pieces_ref, select_ref, back_ref, keep_ref, send_ref, tall
 ):
     tall[...] = pieces_ref[...].astype(F32).reshape(512, 128)
     slots = [tall[pl.ds(slot, 64, stride=8), :].astype(BF) for slot in range(5)]
@@ -168,37 +172,54 @@
     tall[pl.ds(6, 64, stride=8), :] = corner[:, 128:256]
     tall[pl.ds(7, 64, stride=8), :] = corner[:, 0:128]
     back_ref[...] = tall[...].reshape(64, 8, 128).astype(BF)
-    step, core = place_ref[0], place_ref[1]
-
-    def split(at, values):
-        low, high = values[:, 0:128], values[:, 128:256]
-        first_core = core == 0
-        keep_ref[at, :] = jnp.where(first_core, low, high)
-        send_ref[at, :] = jnp.where(first_core, high, low)
-
-    split(pl.ds(0, 1152), grad_ref[...])
+    first_core = place_ref[1] == 0
     for b, values in enumerate((before, first, second)):
-        at = pl.ds(pl.multiple_of(b * step * 128, 128), 128)
         terms = lax.dot_general(
             values.astype(BF), cot, (((0,), (0,)), ((), ())), preferred_element_type=F32
         )
-        split(at, grad_ref[at, :] + terms)
-
-
-def turn_edges(place, pieces, select, grad):
+        keep_ref[b] = jnp.where(first_core, terms[:, 0:128], terms[:, 128:256])
+        send_ref[b] = jnp.where(first_core, terms[:, 128:256], terms[:, 0:128])
+
+
+def turn_edges(place, pieces, select):
     return pl.pallas_call(
         turn_kernel,
-        in_specs=[pl.BlockSpec(memory_space=pltpu.SMEM)] + vmem_specs(3),
+        in_specs=[pl.BlockSpec(memory_space=pltpu.SMEM)] + vmem_specs(2),
         out_specs=vmem_specs(3),
         out_shape=[
             jax.ShapeDtypeStruct((64, 8, 128), BF),
-            jax.ShapeDtypeStruct((1152, 128), F32),
-            jax.ShapeDtypeStruct((1152, 128), F32),
+            jax.ShapeDtypeStruct((3, 128, 128), F32),
+            jax.ShapeDtypeStruct((3, 128, 128), F32),
         ],
         scratch_shapes=[pltpu.VMEM((512, 128), F32)],
         compiler_params=grant(10),
         name="turn_edges",
-    )(place, pieces, select, grad)
+    )(place, pieces, select)
+
+
+def join_and_cut(place, keep, got, edges, got_edges):
+    rows = keep.shape[0] // 4
+
+    def kernel(place_ref, keep_ref, got_ref, edge_ref, got_edge_ref, *refs):
+        total = refs[4]
+        total[...] = keep_ref[...] + got_ref[...]
+        for b in range(3):
+            at = pl.ds(pl.multiple_of(b * place_ref[0] * 128, 128), 128)
+            total[at, :] = total[at, :] + (edge_ref[b] + got_edge_ref[b])
+        own = place_ref[2]
+        for hop in range(4):
+            at = pl.ds(pl.multiple_of(((own + hop) & 3) * rows, rows), rows)
+            refs[hop][...] = total[at, :]
+
+    return pl.pallas_call(
+        kernel,
+        in_specs=[pl.BlockSpec(memory_space=pltpu.SMEM)] + vmem_specs(4),
+        out_specs=vmem_specs(4),
+        out_shape=[jax.ShapeDtypeStruct((rows, 128), F32)] * 4,
+        scratch_shapes=[pltpu.VMEM((4 * rows, 128), F32)],
+        compiler_params=grant(6),
+        name="join_and_cut",
+    )(place, keep, got, edges, got_edges)
 
 
 def sum_and_cut(place, which, parts):
@@ -283,26 +304,35 @@
     rows = mine[0].shape[0]
 
     def kernel(place_ref, *refs):
-        first_core, own = place_ref[1] == 0, place_ref[2]
-        for hop in range(4):
-            at = pl.ds(pl.multiple_of(((own - hop) & 3) * rows, rows), rows)
-            here, there = refs[hop][...], refs[4 + hop][...]
-            refs[8][at, 0:128] = jnp.where(first_core, here, there)
-            refs[8][at, 128:256] = jnp.where(first_core, there, here)
+        core, own = place_ref[1], place_ref[2]
+        out_ref, sems = refs[8], refs[9]
+        copies = []
+        for side in range(2):
+            half = core if side == 0 else 1 - core
+            columns = pl.ds(pl.multiple_of(half * 128, 128), 128)
+            for hop in range(4):
+                at = pl.ds(pl.multiple_of(((own - hop) & 3) * rows, rows), rows)
+                k = 4 * side + hop
+                copies.append(
+                    pltpu.make_async_copy(refs[k], out_ref.at[at, columns], sems.at[k])
+                )
+                copies[-1].start()
+        for copy in copies:
+            copy.wait()
 
     return pl.pallas_call(
         kernel,
         in_specs=[pl.BlockSpec(memory_space=pltpu.SMEM)] + vmem_specs(8),
-        out_specs=vmem_specs(1)[0],
+        out_specs=pl.BlockSpec(memory_space=pl.ANY),
         out_shape=jax.ShapeDtypeStruct((4 * rows, 256), F32),
+        scratch_shapes=[pltpu.SemaphoreType.DMA((8,))],
         compiler_params=grant(6),
         name="final_weights",
     )(place, *mine, *theirs)
 
 
-def tile_kernel(
-    live_ref, act_ref, cot_ref, weight_ref, halo_ref, feat_ref, grad_ref,
-    even, odd, wide, tall, left, line, shift, around, mix, lines,
+def feature_kernel(
+    live_ref, act_ref, weight_ref, halo_ref, feat_ref, even, odd, wide, tall, left, line
 ):
     live = live_ref[0].astype(F32)
     tall[...] = halo_ref[...].astype(F32).reshape(512, 128)
@@ -321,6 +351,35 @@
     result += jnp.dot(even[32:1056, :], weight_ref[768:1152, :], preferred_element_type=F32)
     feat_ref[...] = (result * live).astype(BF).reshape(32, 32, 256)
 
+
+def tile_features(live, act, weight_matrix, halo):
+    return pl.pallas_call(
+        feature_kernel,
+        in_specs=[pl.BlockSpec(memory_space=pltpu.SMEM)] + vmem_specs(3),
+        out_specs=vmem_specs(1)[0],
+        out_shape=jax.ShapeDtypeStruct((32, 32, 256), BF),
+        scratch_shapes=[
+            pltpu.VMEM((1056, 384), BF),
+            pltpu.VMEM((1024, 384), BF),
+            pltpu.VMEM((2, 72, 128), F32),
+            pltpu.VMEM((512, 128), F32),
+            pltpu.VMEM((2, 32, 128), F32),
+            pltpu.VMEM((40, 128), F32),
+        ],
+        cost_estimate=pl.CostEstimate(
+            flops=2 * 1024 * 1152 * 256, bytes_accessed=2 << 20, transcendentals=0
+        ),
+        compiler_params=grant(16),
+        name="tile_features",
+    )(live, act, weight_matrix, halo)
+
+
+def gradient_kernel(
+    live_ref, cot_ref, weight_ref, halo_ref, grad_ref, wide, tall, shift, around, mix, lines
+):
+    live = live_ref[0].astype(F32)
+    tall[...] = halo_ref[...].astype(F32).reshape(512, 128)
+
     right = jnp.concatenate(
         [tall[pl.ds(258, 32, stride=8), :], tall[pl.ds(259, 32, stride=8), :]], axis=1
     )
@@ -381,33 +440,26 @@
     lax.fori_loop(0, 32, weave, 0, unroll=4)
 
 
-def tile_terms(live, act, cot, weight_matrix, halo):
-    return pl.pallas_call(
-        tile_kernel,
-        in_specs=[pl.BlockSpec(memory_space=pltpu.SMEM)] + vmem_specs(4),
-        out_specs=vmem_specs(2),
-        out_shape=[
-            jax.ShapeDtypeStruct((32, 32, 256), BF),
-            jax.ShapeDtypeStruct((64, 64, 128), BF),
-        ],
+def tile_gradient(live, cot, weight_matrix, halo):
+    return pl.pallas_call(
+        gradient_kernel,
+        in_specs=[pl.BlockSpec(memory_space=pltpu.SMEM)] + vmem_specs(3),
+        out_specs=vmem_specs(1)[0],
+        out_shape=jax.ShapeDtypeStruct((64, 64, 128), BF),
         scratch_shapes=[
-            pltpu.VMEM((1056, 384), BF),
-            pltpu.VMEM((1024, 384), BF),
             pltpu.VMEM((2, 72, 128), F32),
             pltpu.VMEM((512, 128), F32),
-            pltpu.VMEM((2, 32, 128), F32),
-            pltpu.VMEM((40, 128), F32),
             pltpu.VMEM((40, 256), F32),
             pltpu.VMEM((40, 256), F32),
             pltpu.VMEM((1056, 512), BF),
             pltpu.VMEM((2, 1024, 256), F32),
         ],
         cost_estimate=pl.CostEstimate(
-            flops=5 * 1024 * 1152 * 256, bytes_accessed=4 << 20, transcendentals=0
+            flops=3 * 1024 * 1152 * 256, bytes_accessed=3 << 20, transcendentals=0
         ),
-        compiler_params=grant(24),
-        name="tile_terms",
-    )(live, act, cot, weight_matrix, halo)
+        compiler_params=grant(20),
+        name="tile_gradient",
+    )(live, cot, weight_matrix, halo)
 
 
 def shards(activations, cotangent, weights, tile_list):
@@ -420,7 +472,7 @@
     live = (lax.dynamic_slice_in_dim(listing, me, 1) >= 0).astype(jnp.int32)
     own = lax.axis_index("slide")
     step = jnp.where(me < slots // 2, 1, 3)
-    place = jnp.stack([step, me & 1, own, (me >> 1) & 3]).astype(jnp.int32)
+    place = jnp.stack([step, me & 1, own, (me >> 1) & 3, live[0]]).astype(jnp.int32)
     select = halo_matrices(listing, me, slots // GW)
     weight_matrix = weights.reshape(-1, weights.shape[3])
 
@@ -435,11 +487,12 @@
         return lax.ppermute(values, "tiles", pairs)
 
     pieces = lax.all_to_all(pack_edges(act, cot), "tiles", 0, 0, tiled=True)
-    inner = interior_weights(live, act, cot)
-    back, keep, send = turn_edges(place, pieces, select, inner)
-
+    keep, send = interior_weights(place, act, cot)
     got = lax.ppermute(send, "tiles", partner)
-    quarters = sum_and_cut(place, 2, [keep, got])
+    back, edges, send_edges = turn_edges(place, pieces, select)
+
+    got_edges = lax.ppermute(send_edges, "tiles", partner)
+    quarters = join_and_cut(place, keep, got, edges, got_edges)
     moved = []
     for hop in range(1, 4):
         moved.append(over_slide(quarters[hop], hop))
@@ -454,9 +507,13 @@
     grad_scale = 1.0 / math.sqrt(slides * slots * half_side * half_side)
     eighth = sum_scaled(parts, grad_scale)
 
-    features_out, input_grad = tile_terms(live, act, cot, weight_matrix, halo)
-
-    quarter = assemble(place, 3, [eighth] + [over_x(eighth, hop) for hop in range(1, 4)])
+    features_out = tile_features(live, act, weight_matrix, halo)
+    input_grad = tile_gradient(live, cot, weight_matrix, halo)
+
+    eighths = [eighth]
+    for hop in range(1, 4):
+        eighths.append(over_x(eighth, hop))
+    quarter = assemble(place, 3, eighths)
     mine = [quarter]
     for hop in range(1, 4):
         mine.append(over_slide(quarter, hop))

time: 101 us -> 98.5 us (0.975)
  local copies, waits for them, and re-layouts: 1.86 us -> 0.11 us
  waiting for transfers between devices: 19 us -> 17.7 us
    unnamed x16 -> x8, local copies, waits for them, and re-layouts: 1.86 us -> 0.02 us
    pallas_call x1, Pallas kernels: 1.25 us -> 2.61 us  [interior_weights(): pl.pallas_call(weight_kernel, in_specs=[pl.BlockSpec(memory_space=pltpu.S...]
    all_to_all x1, waiting for transfers between devices: 7.41 us -> 6.13 us  [shards(): pieces = lax.all_to_all(pack_edges(act, cot), 'tiles', 0, 0, tiled=True)]
    pallas_call x1 -> x3, Pallas kernels: 5.78 us -> 5.55 us  [the longest x1 2.64 us: tile_gradient(): pl.pallas_call(gradient_kernel, in_specs=[pl.BlockSpec(memory_space=pltpu...]
  transfers between devices with their start and end apart: 19 -> 20, of which waited for: 7 -> 7; matrix products, arithmetic and copies ran while one was open for 2% -> 1% of each run, Pallas kernels for 8% -> 11%
where the time goes in v1:
time: 98.5 us; the launch traced here: 98.3 us
  starting transfers between devices  47.3 us (48%)
  waiting for transfers between devices  17.7 us (18%)
  blocking collectives  15.9 us (16%)
  Pallas kernels  14.5 us (15%)
  between operations  1.64 us (2%)
  other arithmetic  1.09 us (1%)
    all_to_all x1, blocking collectives, shards(): lax.all_to_all(copies, 'tiles', 0, 0, tiled=True, axis_index_groups=columns)  15.9 us
    all_to_all x1, starting transfers between devices, shards(): pieces = lax.all_to_all(pack_edges(act, cot), 'tiles', 0, 0, tiled=True)  13 us
    ppermute x4, starting transfers between devices, shards(): theirs.append(lax.ppermute(mine[hop], 'tiles', partner))  12.7 us
    ppermute x6, starting transfers between devices, over_x(): return lax.ppermute(values, 'tiles', pairs)  8.29 us
    ppermute x6, starting transfers between devices, over_slide(): lax.ppermute(values, 'slide', [(i, (i + hop) % slides) for i in range(sli...  8.25 us
    all_to_all x1, waiting for transfers between devices, shards(): pieces = lax.all_to_all(pack_edges(act, cot), 'tiles', 0, 0, tiled=True)  6.13 us
    ppermute x6, waiting for transfers between devices, over_x(): return lax.ppermute(values, 'tiles', pairs)  6.06 us
    ppermute x6, waiting for transfers between devices, over_slide(): lax.ppermute(values, 'slide', [(i, (i + hop) % slides) for i in range(sli...  5.49 us
  transfers between devices with their start and end apart: 20, of which 7 were waited for; matrix products, arithmetic and copies ran while one was open for 1% of the time, Pallas kernels for 11%

profile of v1, /device:TPU:1, one launch (start us, length us, event | category | flops | bytes accessed | tf_op | source)
XLA Modules:
  0.0 98.3 jit_solution(16037417498199569983)
XLA Ops:
  0.7 1.9 %pack_edges.1 = bf16[64,8,128]{2,1,0:T(8,128)(2,1)} custom-call(bf16[64,64,128]{2,1,0:T(8,128)(2,1)} %bitcast.35, bf16[32,32,256]{2,1,0:T(8,128)(2,1)} %bitcast.40), custom_call_target="tpu_custom_call" | custom-call | tf_op jit(solution)/shard_map/pack_edges/pallas_call | solution.py:79
  2.6 13.0 %all-to-all-start = ((bf16[64,8,128]{2,1,0:T(8,128)(2,1)}), bf16[64,8,128]{2,1,0:T(8,128)(2,1)S(1)}, u32[]{:S(2)}, u32[]{:S(2)}) async-start(bf16[64,8,128]{2,1,0:T(8,128)(2,1)} %pack_edges.1), calls=%async_computation | async-start | bytes 262144 | tf_op jit(solution)/shard_map/all_to_all | solution.py:489
  15.6 0.6 fusion.2
  16.8 0.1 stack.27.place_ref
  16.9 2.6 %interior_weights.1 = (f32[1152,128]{1,0:T(8,128)S(1)}, f32[1152,128]{1,0:T(8,128)}) custom-call(s32[5]{0:T(128)S(1)} %stack.27.place_ref, bf16[64,64,128]{2,1,0:T(8,128)(2,1)S(1)} %bitcast.36, bf16[32,32,256]{2,1,0:T(8,128)(2,1)S(1)} %bitcast.41), custom_call_target="tpu_custom_call" | custom-call | flops 603979776 | bytes 3145728 | tf_op jit(solution)/shard_map/interior_weights/pallas_call | solution.py:135
  19.5 0.5 collective-permute-start
  20.0 0.1 fusion
  20.1 0.1 fusion.1
  20.2 0.1 select_dynamic-update-slice_fusion
  20.3 0.1 compare_dynamic-update-slice_fusion
  20.4 0.1 compare_dynamic-update-slice_fusion.1
  20.5 6.1 %all-to-all-done.pieces_ref = bf16[64,8,128]{2,1,0:T(8,128)(2,1)S(1)} async-done(((bf16[64,8,128]{2,1,0:T(8,128)(2,1)}), bf16[64,8,128]{2,1,0:T(8,128)(2,1)S(1)}, u32[]{:S(2)}, u32[]{:S(2)}) %all-to-all-start) | async-done | bytes 131104 | tf_op jit(solution)/shard_map/all_to_all | solution.py:489
  26.7 1.6 %turn_edges.1 = (bf16[64,8,128]{2,1,0:T(8,128)(2,1)}, f32[3,128,128]{2,1,0:T(8,128)S(1)}, f32[3,128,128]{2,1,0:T(8,128)}) custom-call(s32[5]{0:T(128)S(1)} %stack.27.place_ref, bf16[64,8,128]{2,1,0:T(8,128)(2,1)S(1)} %all-to-all-done.pieces_ref, bf16[5,64,64]{2,1,0:T(8,128)(2,1)S(1)} %convert_element_type.10.select_ref), custom_call_target="tpu_custom_call" | custom-call | tf_op jit(solution)/shard_map/turn_edges/pallas_call | solution.py:185
  28.3 0.4 collective-permute-start.1
  28.7 4.2 %all-to-all-start.1 = ((bf16[64,8,128]{2,1,0:T(8,128)(2,1)}), bf16[64,8,128]{2,1,0:T(8,128)(2,1)S(1)}, u32[]{:S(2)}, u32[]{:S(2)}) async-start(bf16[64,8,128]{2,1,0:T(8,128)(2,1)} %get-tuple-element.30), calls=%async_computation.1 | async-start | bytes 262144 | tf_op jit(solution)/shard_map/all_to_all | solution.py:499
  32.9 0.0 collective-permute-done.1.got_edge_ref
  32.9 0.0 collective-permute-done.got_ref
  32.9 0.7 join_and_cut.1
  33.6 0.0 copy-start.1
  33.6 1.4 %collective-permute-start.2 = (f32[288,128]{1,0:T(8,128)S(1)}, f32[288,128]{1,0:T(8,128)S(1)}, u32[]{:S(2)}, u32[]{:S(2)}) collective-permute-start(f32[288,128]{1,0:T(8,128)S(1)} %get-tuple-element.23), channel_id=1, source_target_pairs={{0,1},{1,2},{2,3},{3,0},{4,5},{5,6},{6,7},{7,4},{8,9},{9,10},{10,1... | collective-permute-start | bytes 442376 | tf_op jit(solution)/shard_map/ppermute | solution.py:483
  35.0 2.6 %collective-permute-start.3 = (f32[288,128]{1,0:T(8,128)S(1)}, f32[288,128]{1,0:T(8,128)S(1)}, u32[]{:S(2)}, u32[]{:S(2)}) collective-permute-start(f32[288,128]{1,0:T(8,128)S(1)} %get-tuple-element.24), channel_id=1, source_target_pairs={{0,2},{1,3},{2,0},{3,1},{4,6},{5,7},{6,4},{7,5},{8,10},{9,11},{10,... | collective-permute-start | bytes 442376 | tf_op jit(solution)/shard_map/ppermute | solution.py:483
  37.6 1.1 %collective-permute-start.4 = (f32[288,128]{1,0:T(8,128)S(1)}, f32[288,128]{1,0:T(8,128)S(1)}, u32[]{:S(2)}, u32[]{:S(2)}) collective-permute-start(f32[288,128]{1,0:T(8,128)S(1)} %get-tuple-element.25), channel_id=1, source_target_pairs={{0,3},{1,0},{2,1},{3,2},{4,7},{5,4},{6,5},{7,6},{8,11},{9,8},{10,9... | collective-permute-start | bytes 442376 | tf_op jit(solution)/shard_map/ppermute | solution.py:483
  38.7 1.2 %collective-permute-done.2.refs_1_ = f32[288,128]{1,0:T(8,128)S(1)} collective-permute-done((f32[288,128]{1,0:T(8,128)S(1)}, f32[288,128]{1,0:T(8,128)S(1)}, u32[]{:S(2)}, u32[]{:S(2)}) %collective-permute-start.2) | collective-permute-done | bytes 147488 | tf_op jit(solution)/shard_map/ppermute | solution.py:483
  39.9 4.3 %collective-permute-done.3.refs_2_ = f32[288,128]{1,0:T(8,128)S(1)} collective-permute-done((f32[288,128]{1,0:T(8,128)S(1)}, f32[288,128]{1,0:T(8,128)S(1)}, u32[]{:S(2)}, u32[]{:S(2)}) %collective-permute-start.3) | collective-permute-done | bytes 147488 | tf_op jit(solution)/shard_map/ppermute | solution.py:483
  44.1 0.0 collective-permute-done.4.refs_3_
  44.1 0.6 sum_and_cut.1
  44.7 1.6 %collective-permute-start.5 = (f32[72,128]{1,0:T(8,128)S(1)}, f32[72,128]{1,0:T(8,128)S(1)}, u32[]{:S(2)}, u32[]{:S(2)}) collective-permute-start(f32[72,128]{1,0:T(8,128)S(1)} %get-tuple-element.27), channel_id=1, source_target_pairs={{0,8},{4,12},{8,16},{12,20},{16,24},{20,28},{24,0},{28,4},{32,40},... | collective-permute-start | bytes 110600 | tf_op jit(solution)/shard_map/ppermute | solution.py:487
  46.3 2.4 %collective-permute-start.6 = (f32[72,128]{1,0:T(8,128)S(1)}, f32[72,128]{1,0:T(8,128)S(1)}, u32[]{:S(2)}, u32[]{:S(2)}) collective-permute-start(f32[72,128]{1,0:T(8,128)S(1)} %get-tuple-element.28), channel_id=1, source_target_pairs={{0,16},{4,20},{8,24},{12,28},{16,0},{20,4},{24,8},{28,12},{32,48},... | collective-permute-start | bytes 110600 | tf_op jit(solution)/shard_map/ppermute | solution.py:487
  48.7 1.2 %collective-permute-start.7 = (f32[72,128]{1,0:T(8,128)S(1)}, f32[72,128]{1,0:T(8,128)S(1)}, u32[]{:S(2)}, u32[]{:S(2)}) collective-permute-start(f32[72,128]{1,0:T(8,128)S(1)} %get-tuple-element.29), channel_id=1, source_target_pairs={{0,24},{4,28},{8,0},{12,4},{16,8},{20,12},{24,16},{28,20},{32,56},... | collective-permute-start | bytes 110600 | tf_op jit(solution)/shard_map/ppermute | solution.py:487
  49.9 0.8 collective-permute-done.6.refs_2_
  50.7 1.6 %collective-permute-done.7.refs_3_ = f32[72,128]{1,0:T(8,128)S(1)} collective-permute-done((f32[72,128]{1,0:T(8,128)S(1)}, f32[72,128]{1,0:T(8,128)S(1)}, u32[]{:S(2)}, u32[]{:S(2)}) %collective-permute-start.7) | collective-permute-done | bytes 36896 | tf_op jit(solution)/shard_map/ppermute | solution.py:487
  52.3 15.9 %all_to_all.15.parts_ref = f32[8,72,128]{2,1,0:T(8,128)S(1)} all-to-all(f32[8,72,128]{2,1,0:T(8,128)S(1)} %shard_map.67), channel_id=1, replica_groups={{0,32,64,96,128,160,192,224},{4,36,68,100,132,164,196,228},{8,40,72,104..., dimensions={0} | all-to-all | bytes 589824 | tf_op jit(solution)/shard_map/all_to_all | solution.py:506
  68.2 2.4 %collective-permute-start.10 = (f32[72,128]{1,0:T(8,128)S(1)}, f32[72,128]{1,0:T(8,128)S(1)}, u32[]{:S(2)}, u32[]{:S(2)}) collective-permute-start(f32[72,128]{1,0:T(8,128)S(1)} %sum_scaled.1.refs_0_), channel_id=1, source_target_pairs={{0,24},{4,28},{8,0},{12,4},{16,8},{20,12},{24,16},{28,20},{32,56},... | collective-permute-start | bytes 110600 | tf_op jit(solution)/shard_map/ppermute | solution.py:487
  70.7 0.7 collective-permute-start.8
  71.3 0.4 collective-permute-done.10.refs_3_
  71.7 3.3 %collective-permute-done.9.refs_2_ = f32[72,128]{1,0:T(8,128)S(1)} collective-permute-done((f32[72,128]{1,0:T(8,128)S(1)}, f32[72,128]{1,0:T(8,128)S(1)}, u32[]{:S(2)}, u32[]{:S(2)}) %collective-permute-start.9) | collective-permute-done | bytes 36896 | tf_op jit(solution)/shard_map/ppermute | solution.py:487
  75.1 0.0 collective-permute-done.8.refs_1_
  75.1 0.6 assemble.1.refs_0_
  75.6 2.3 %collective-permute-start.13 = (f32[288,128]{1,0:T(8,128)S(1)}, f32[288,128]{1,0:T(8,128)S(1)}, u32[]{:S(2)}, u32[]{:S(2)}) collective-permute-start(f32[288,128]{1,0:T(8,128)S(1)} %assemble.1.refs_0_), channel_id=1, source_target_pairs={{0,3},{1,0},{2,1},{3,2},{4,7},{5,4},{6,5},{7,6},{8,11},{9,8},{10,9... | collective-permute-start | bytes 442376 | tf_op jit(solution)/shard_map/ppermute | solution.py:483
  78.0 0.8 collective-permute-start.12
  78.7 0.1 collective-permute-start.11
  78.8 6.2 %collective-permute-start.14 = (f32[288,128]{1,0:T(8,128)S(1)}, f32[288,128]{1,0:T(8,128)S(1)}, u32[]{:S(2)}, u32[]{:S(2)}) collective-permute-start(f32[288,128]{1,0:T(8,128)S(1)} %assemble.1.refs_0_), channel_id=1, source_target_pairs={{0,4},{4,0},{8,12},{12,8},{16,20},{20,16},{24,28},{28,24},{32,36},... | collective-permute-start | bytes 442376 | tf_op jit(solution)/shard_map/ppermute | solution.py:522
  85.0 2.6 %collective-permute-start.17 = (f32[288,128]{1,0:T(8,128)S(1)}, f32[288,128]{1,0:T(8,128)S(1)}, u32[]{:S(2)}, u32[]{:S(2)}) collective-permute-start(f32[288,128]{1,0:T(8,128)S(1)} %collective-permute-done.13.refs_3_), channel_id=1, source_target_pairs={{0,4},{4,0},{8,12},{12,8},{16,20},{20,16},{24,28},{28,24},{32,36},... | collective-permute-start | bytes 442376 | tf_op jit(solution)/shard_map/ppermute | solution.py:522
  87.6 2.5 %collective-permute-start.16 = (f32[288,128]{1,0:T(8,128)S(1)}, f32[288,128]{1,0:T(8,128)S(1)}, u32[]{:S(2)}, u32[]{:S(2)}) collective-permute-start(f32[288,128]{1,0:T(8,128)S(1)} %collective-permute-done.12.refs_2_), channel_id=1, source_target_pairs={{0,4},{4,0},{8,12},{12,8},{16,20},{20,16},{24,28},{28,24},{32,36},... | collective-permute-start | bytes 442376 | tf_op jit(solution)/shard_map/ppermute | solution.py:522
  90.1 1.5 %collective-permute-start.15 = (f32[288,128]{1,0:T(8,128)S(1)}, f32[288,128]{1,0:T(8,128)S(1)}, u32[]{:S(2)}, u32[]{:S(2)}) collective-permute-start(f32[288,128]{1,0:T(8,128)S(1)} %collective-permute-done.11.refs_1_), channel_id=1, source_target_pairs={{0,4},{4,0},{8,12},{12,8},{16,20},{20,16},{24,28},{28,24},{32,36},... | collective-permute-start | bytes 442376 | tf_op jit(solution)/shard_map/ppermute | solution.py:522
  91.6 2.2 %tile_features.1 = bf16[32,32,256]{2,1,0:T(8,128)(2,1)} custom-call(s32[1]{0:T(128)} %bitcast.live_ref, bf16[64,64,128]{2,1,0:T(8,128)(2,1)S(1)} %bitcast.37, bf16[1152,256]{1,0:T(8,128)(2,1)S(1)} %bitcast.38, bf16[64,8,128]{2,1,0:T(8,128)(2,1)S(1)} %all-to-all-done.1.halo_ref), custom_call_target="tpu_custom_call" | custom-call | flops 603979776 | bytes 2097152 | tf_op jit(solution)/shard_map/tile_features/pallas_call | solution.py:356
  93.8 2.6 %tile_gradient.1 = bf16[64,64,128]{2,1,0:T(8,128)(2,1)} custom-call(s32[1]{0:T(128)} %bitcast.live_ref, bf16[32,32,256]{2,1,0:T(8,128)(2,1)S(1)} %bitcast.42, bf16[1152,256]{1,0:T(8,128)(2,1)S(1)} %bitcast.39, bf16[64,8,128]{2,1,0:T(8,128)(2,1)S(1)} %all-to-all-done.1.halo_ref), custom_call_target="tpu_custom_call" | custom-call | flops 905969664 | bytes 3145728 | tf_op jit(solution)/shard_map/tile_gradient/pallas_call | solution.py:444
  96.5 1.6 %final_weights.1 = f32[1152,256]{1,0:T(8,128)} custom-call(s32[5]{0:T(128)S(1)} %stack.27.place_ref, f32[288,128]{1,0:T(8,128)S(1)} %assemble.1.refs_0_, f32[288,128]{1,0:T(8,128)S(1)} %collective-permute-done.11.refs_1_, f32[288,128]{1,0:T(8,128)S(1)} %collective-permute-done.12.refs_2_, f32[288,128]{1,0:T(8,128)S(1)} %collective-permute-done.13.refs_3_, ...), custom_call_target="tpu_custom_call" | custom-call | tf_op jit(solution)/shard_map/final_weights/pallas_call | solution.py:323
  (22 shorter events, 0.1 us)
Async XLA Ops:
  0.6 16.3 %copy-start.2 = (bf16[1,1,32,32,256]{4,3,2,1,0:T(8,128)(2,1)S(1)}, bf16[1,1,32,32,256]{4,3,2,1,0:T(8,128)(2,1)}, u32[]{:S(2)}) copy-start(bf16[1,1,32,32,256]{4,3,2,1,0:T(8,128)(2,1)} %param.5) | copy-start | bytes 1572868
  0.6 16.3 %copy-start = (bf16[1,1,64,64,128]{4,3,2,1,0:T(8,128)(2,1)S(1)}, bf16[1,1,64,64,128]{4,3,2,1,0:T(8,128)(2,1)}, u32[]{:S(2)}) copy-start(bf16[1,1,64,64,128]{4,3,2,1,0:T(8,128)(2,1)} %param.4) | copy-start | bytes 3145732
  0.7 14.9 %copy-start.3 = (s32[1,64]{1,0:T(1,128)S(1)}, s32[1,64]{1,0:T(1,128)}, u32[]{:S(2)}) copy-start(s32[1,64]{1,0:T(1,128)} %param.7) | copy-start | bytes 772
  2.6 24.1 %all-to-all-start = ((bf16[64,8,128]{2,1,0:T(8,128)(2,1)}), bf16[64,8,128]{2,1,0:T(8,128)(2,1)S(1)}, u32[]{:S(2)}, u32[]{:S(2)}) async-start(bf16[64,8,128]{2,1,0:T(8,128)(2,1)} %pack_edges.1), calls=%async_computation | async-start | bytes 262144 | tf_op jit(solution)/shard_map/all_to_all | solution.py:489
  19.5 13.4 %collective-permute-start = (f32[1152,128]{1,0:T(8,128)}, f32[1152,128]{1,0:T(8,128)S(1)}, u32[]{:S(2)}, u32[]{:S(2)}) collective-permute-start(f32[1152,128]{1,0:T(8,128)} %get-tuple-element.19), channel_id=1, source_target_pairs={{0,4},{4,0},{8,12},{12,8},{16,20},{20,16},{24,28},{28,24},{32,36},... | collective-permute-start | bytes 1769480 | tf_op jit(solution)/shard_map/ppermute | solution.py:491
  28.3 4.6 %collective-permute-start.1 = (f32[3,128,128]{2,1,0:T(8,128)}, f32[3,128,128]{2,1,0:T(8,128)S(1)}, u32[]{:S(2)}, u32[]{:S(2)}) collective-permute-start(f32[3,128,128]{2,1,0:T(8,128)} %get-tuple-element.21), channel_id=1, source_target_pairs={{0,4},{4,0},{8,12},{12,8},{16,20},{20,16},{24,28},{28,24},{32,36},... | collective-permute-start | bytes 589832 | tf_op jit(solution)/shard_map/ppermute | solution.py:494
  28.7 23.6 %all-to-all-start.1 = ((bf16[64,8,128]{2,1,0:T(8,128)(2,1)}), bf16[64,8,128]{2,1,0:T(8,128)(2,1)S(1)}, u32[]{:S(2)}, u32[]{:S(2)}) async-start(bf16[64,8,128]{2,1,0:T(8,128)(2,1)} %get-tuple-element.30), calls=%async_computation.1 | async-start | bytes 262144 | tf_op jit(solution)/shard_map/all_to_all | solution.py:499
  33.6 58.0 %copy-start.1 = (bf16[3,3,128,256]{3,2,1,0:T(8,128)(2,1)S(1)}, bf16[3,3,128,256]{3,2,1,0:T(8,128)(2,1)}, u32[]{:S(2)}) copy-start(bf16[3,3,128,256]{3,2,1,0:T(8,128)(2,1)} %param.6) | copy-start | bytes 1769476
  33.6 6.3 %collective-permute-start.2 = (f32[288,128]{1,0:T(8,128)S(1)}, f32[288,128]{1,0:T(8,128)S(1)}, u32[]{:S(2)}, u32[]{:S(2)}) collective-permute-start(f32[288,128]{1,0:T(8,128)S(1)} %get-tuple-element.23), channel_id=1, source_target_pairs={{0,1},{1,2},{2,3},{3,0},{4,5},{5,6},{6,7},{7,4},{8,9},{9,10},{10,1... | collective-permute-start | bytes 442376 | tf_op jit(solution)/shard_map/ppermute | solution.py:483
  35.0 9.2 %collective-permute-start.3 = (f32[288,128]{1,0:T(8,128)S(1)}, f32[288,128]{1,0:T(8,128)S(1)}, u32[]{:S(2)}, u32[]{:S(2)}) collective-permute-start(f32[288,128]{1,0:T(8,128)S(1)} %get-tuple-element.24), channel_id=1, source_target_pairs={{0,2},{1,3},{2,0},{3,1},{4,6},{5,7},{6,4},{7,5},{8,10},{9,11},{10,... | collective-permute-start | bytes 442376 | tf_op jit(solution)/shard_map/ppermute | solution.py:483
  37.6 6.6 %collective-permute-start.4 = (f32[288,128]{1,0:T(8,128)S(1)}, f32[288,128]{1,0:T(8,128)S(1)}, u32[]{:S(2)}, u32[]{:S(2)}) collective-permute-start(f32[288,128]{1,0:T(8,128)S(1)} %get-tuple-element.25), channel_id=1, source_target_pairs={{0,3},{1,0},{2,1},{3,2},{4,7},{5,4},{6,5},{7,6},{8,11},{9,8},{10,9... | collective-permute-start | bytes 442376 | tf_op jit(solution)/shard_map/ppermute | solution.py:483
  44.7 5.2 %collective-permute-start.5 = (f32[72,128]{1,0:T(8,128)S(1)}, f32[72,128]{1,0:T(8,128)S(1)}, u32[]{:S(2)}, u32[]{:S(2)}) collective-permute-start(f32[72,128]{1,0:T(8,128)S(1)} %get-tuple-element.27), channel_id=1, source_target_pairs={{0,8},{4,12},{8,16},{12,20},{16,24},{20,28},{24,0},{28,4},{32,40},... | collective-permute-start | bytes 110600 | tf_op jit(solution)/shard_map/ppermute | solution.py:487
  46.3 4.3 %collective-permute-start.6 = (f32[72,128]{1,0:T(8,128)S(1)}, f32[72,128]{1,0:T(8,128)S(1)}, u32[]{:S(2)}, u32[]{:S(2)}) collective-permute-start(f32[72,128]{1,0:T(8,128)S(1)} %get-tuple-element.28), channel_id=1, source_target_pairs={{0,16},{4,20},{8,24},{12,28},{16,0},{20,4},{24,8},{28,12},{32,48},... | collective-permute-start | bytes 110600 | tf_op jit(solution)/shard_map/ppermute | solution.py:487
  48.7 3.5 %collective-permute-start.7 = (f32[72,128]{1,0:T(8,128)S(1)}, f32[72,128]{1,0:T(8,128)S(1)}, u32[]{:S(2)}, u32[]{:S(2)}) collective-permute-start(f32[72,128]{1,0:T(8,128)S(1)} %get-tuple-element.29), channel_id=1, source_target_pairs={{0,24},{4,28},{8,0},{12,4},{16,8},{20,12},{24,16},{28,20},{32,56},... | collective-permute-start | bytes 110600 | tf_op jit(solution)/shard_map/ppermute | solution.py:487
  68.2 3.5 %collective-permute-start.10 = (f32[72,128]{1,0:T(8,128)S(1)}, f32[72,128]{1,0:T(8,128)S(1)}, u32[]{:S(2)}, u32[]{:S(2)}) collective-permute-start(f32[72,128]{1,0:T(8,128)S(1)} %sum_scaled.1.refs_0_), channel_id=1, source_target_pairs={{0,24},{4,28},{8,0},{12,4},{16,8},{20,12},{24,16},{28,20},{32,56},... | collective-permute-start | bytes 110600 | tf_op jit(solution)/shard_map/ppermute | solution.py:487
  70.7 4.4 %collective-permute-start.9 = (f32[72,128]{1,0:T(8,128)S(1)}, f32[72,128]{1,0:T(8,128)S(1)}, u32[]{:S(2)}, u32[]{:S(2)}) collective-permute-start(f32[72,128]{1,0:T(8,128)S(1)} %sum_scaled.1.refs_0_), channel_id=1, source_target_pairs={{0,16},{4,20},{8,24},{12,28},{16,0},{20,4},{24,8},{28,12},{32,48},... | collective-permute-start | bytes 110600 | tf_op jit(solution)/shard_map/ppermute | solution.py:487
  70.7 4.4 %collective-permute-start.8 = (f32[72,128]{1,0:T(8,128)S(1)}, f32[72,128]{1,0:T(8,128)S(1)}, u32[]{:S(2)}, u32[]{:S(2)}) collective-permute-start(f32[72,128]{1,0:T(8,128)S(1)} %sum_scaled.1.refs_0_), channel_id=1, source_target_pairs={{0,8},{4,12},{8,16},{12,20},{16,24},{20,28},{24,0},{28,4},{32,40},... | collective-permute-start | bytes 110600 | tf_op jit(solution)/shard_map/ppermute | solution.py:487
  75.6 9.4 %collective-permute-start.13 = (f32[288,128]{1,0:T(8,128)S(1)}, f32[288,128]{1,0:T(8,128)S(1)}, u32[]{:S(2)}, u32[]{:S(2)}) collective-permute-start(f32[288,128]{1,0:T(8,128)S(1)} %assemble.1.refs_0_), channel_id=1, source_target_pairs={{0,3},{1,0},{2,1},{3,2},{4,7},{5,4},{6,5},{7,6},{8,11},{9,8},{10,9... | collective-permute-start | bytes 442376 | tf_op jit(solution)/shard_map/ppermute | solution.py:483
  78.0 9.7 %collective-permute-start.12 = (f32[288,128]{1,0:T(8,128)S(1)}, f32[288,128]{1,0:T(8,128)S(1)}, u32[]{:S(2)}, u32[]{:S(2)}) collective-permute-start(f32[288,128]{1,0:T(8,128)S(1)} %assemble.1.refs_0_), channel_id=1, source_target_pairs={{0,2},{1,3},{2,0},{3,1},{4,6},{5,7},{6,4},{7,5},{8,10},{9,11},{10,... | collective-permute-start | bytes 442376 | tf_op jit(solution)/shard_map/ppermute | solution.py:483
  78.7 11.3 %collective-permute-start.11 = (f32[288,128]{1,0:T(8,128)S(1)}, f32[288,128]{1,0:T(8,128)S(1)}, u32[]{:S(2)}, u32[]{:S(2)}) collective-permute-start(f32[288,128]{1,0:T(8,128)S(1)} %assemble.1.refs_0_), channel_id=1, source_target_pairs={{0,1},{1,2},{2,3},{3,0},{4,5},{5,6},{6,7},{7,4},{8,9},{9,10},{10,1... | collective-permute-start | bytes 442376 | tf_op jit(solution)/shard_map/ppermute | solution.py:483
  78.8 17.6 %collective-permute-start.14 = (f32[288,128]{1,0:T(8,128)S(1)}, f32[288,128]{1,0:T(8,128)S(1)}, u32[]{:S(2)}, u32[]{:S(2)}) collective-permute-start(f32[288,128]{1,0:T(8,128)S(1)} %assemble.1.refs_0_), channel_id=1, source_target_pairs={{0,4},{4,0},{8,12},{12,8},{16,20},{20,16},{24,28},{28,24},{32,36},... | collective-permute-start | bytes 442376 | tf_op jit(solution)/shard_map/ppermute | solution.py:522
  85.0 11.4 %collective-permute-start.17 = (f32[288,128]{1,0:T(8,128)S(1)}, f32[288,128]{1,0:T(8,128)S(1)}, u32[]{:S(2)}, u32[]{:S(2)}) collective-permute-start(f32[288,128]{1,0:T(8,128)S(1)} %collective-permute-done.13.refs_3_), channel_id=1, source_target_pairs={{0,4},{4,0},{8,12},{12,8},{16,20},{20,16},{24,28},{28,24},{32,36},... | collective-permute-start | bytes 442376 | tf_op jit(solution)/shard_map/ppermute | solution.py:522
  87.6 8.8 %collective-permute-start.16 = (f32[288,128]{1,0:T(8,128)S(1)}, f32[288,128]{1,0:T(8,128)S(1)}, u32[]{:S(2)}, u32[]{:S(2)}) collective-permute-start(f32[288,128]{1,0:T(8,128)S(1)} %collective-permute-done.12.refs_2_), channel_id=1, source_target_pairs={{0,4},{4,0},{8,12},{12,8},{16,20},{20,16},{24,28},{28,24},{32,36},... | collective-permute-start | bytes 442376 | tf_op jit(solution)/shard_map/ppermute | solution.py:522
  90.1 6.4 %collective-permute-start.15 = (f32[288,128]{1,0:T(8,128)S(1)}, f32[288,128]{1,0:T(8,128)S(1)}, u32[]{:S(2)}, u32[]{:S(2)}) collective-permute-start(f32[288,128]{1,0:T(8,128)S(1)} %collective-permute-done.11.refs_1_), channel_id=1, source_target_pairs={{0,4},{4,0},{8,12},{12,8},{16,20},{20,16},{24,28},{28,24},{32,36},... | collective-permute-start | bytes 442376 | tf_op jit(solution)/shard_map/ppermute | solution.py:522

commit v2 on v1

--- a/solution.py
+++ b/solution.py
@@ -91,6 +91,7 @@
             pltpu.VMEM((72, 128), F32),
             pltpu.VMEM((512, 128), F32),
         ],
+        compiler_params=grant(60),
         name="pack_edges",
     )(act, cot)
 
@@ -150,51 +151,63 @@
     )(place, act, cot)
 
 
-def turn_kernel(
-    place_ref, pieces_ref, select_ref, back_ref, keep_ref, send_ref, tall
-):
+def pick(select, values):
+    return jnp.dot(select, values, preferred_element_type=F32)
+
+
+def edge_kernel(place_ref, pieces_ref, select_ref, keep_ref, send_ref, tall):
     tall[...] = pieces_ref[...].astype(F32).reshape(512, 128)
     slots = [tall[pl.ds(slot, 64, stride=8), :].astype(BF) for slot in range(5)]
     cot = jnp.concatenate(slots[3:5], axis=1)
-
-    def pick(which, values):
-        return jnp.dot(select_ref[which], values, preferred_element_type=F32)
-
-    before, first, second = pick(0, slots[0]), pick(1, slots[1]), pick(1, slots[2])
-    returned = pick(2, cot)
-    corner = pick(4, cot)
-    tall[pl.ds(0, 64, stride=8), :] = first
-    tall[pl.ds(1, 64, stride=8), :] = second
+    first_core = place_ref[1] == 0
+    for b in range(3):
+        values = pick(select_ref[min(b, 1)], slots[b]).astype(BF)
+        terms = lax.dot_general(
+            values, cot, (((0,), (0,)), ((), ())), preferred_element_type=F32
+        )
+        keep_ref[b] = jnp.where(first_core, terms[:, 0:128], terms[:, 128:256])
+        send_ref[b] = jnp.where(first_core, terms[:, 128:256], terms[:, 0:128])
+
+
+def edge_weights(place, pieces, select):
+    return pl.pallas_call(
+        edge_kernel,
+        in_specs=[pl.BlockSpec(memory_space=pltpu.SMEM)] + vmem_specs(2),
+        out_specs=vmem_specs(2),
+        out_shape=[jax.ShapeDtypeStruct((3, 128, 128), F32)] * 2,
+        scratch_shapes=[pltpu.VMEM((512, 128), F32)],
+        compiler_params=grant(6),
+        name="edge_weights",
+    )(place, pieces, select)
+
+
+def turn_kernel(pieces_ref, select_ref, back_ref, tall):
+    tall[...] = pieces_ref[...].astype(F32).reshape(512, 128)
+    slots = [tall[pl.ds(slot, 64, stride=8), :].astype(BF) for slot in range(5)]
+    cot = jnp.concatenate(slots[3:5], axis=1)
+    returned = pick(select_ref[2], cot)
+    corner = pick(select_ref[4], cot)
+    tall[pl.ds(0, 64, stride=8), :] = pick(select_ref[1], slots[1])
+    tall[pl.ds(1, 64, stride=8), :] = pick(select_ref[1], slots[2])
     tall[pl.ds(2, 64, stride=8), :] = returned[:, 0:128]
     tall[pl.ds(3, 64, stride=8), :] = returned[:, 128:256]
-    tall[pl.ds(4, 64, stride=8), :] = pick(3, slots[0])
+    tall[pl.ds(4, 64, stride=8), :] = pick(select_ref[3], slots[0])
     tall[pl.ds(5, 64, stride=8), :] = corner[:, 0:128]
     tall[pl.ds(6, 64, stride=8), :] = corner[:, 128:256]
     tall[pl.ds(7, 64, stride=8), :] = corner[:, 0:128]
     back_ref[...] = tall[...].reshape(64, 8, 128).astype(BF)
-    first_core = place_ref[1] == 0
-    for b, values in enumerate((before, first, second)):
-        terms = lax.dot_general(
-            values.astype(BF), cot, (((0,), (0,)), ((), ())), preferred_element_type=F32
-        )
-        keep_ref[b] = jnp.where(first_core, terms[:, 0:128], terms[:, 128:256])
-        send_ref[b] = jnp.where(first_core, terms[:, 128:256], terms[:, 0:128])
-
-
-def turn_edges(place, pieces, select):
+
+
+def turn_edges(pieces, select):
     return pl.pallas_call(
         turn_kernel,
-        in_specs=[pl.BlockSpec(memory_space=pltpu.SMEM)] + vmem_specs(2),
-        out_specs=vmem_specs(3),
-        out_shape=[
-            jax.ShapeDtypeStruct((64, 8, 128), BF),
-            jax.ShapeDtypeStruct((3, 128, 128), F32),
-            jax.ShapeDtypeStruct((3, 128, 128), F32),
-        ],
+        in_specs=vmem_specs(2),
+        out_specs=vmem_specs(1)[0],
+        out_shape=jax.ShapeDtypeStruct((64, 8, 128), BF),
         scratch_shapes=[pltpu.VMEM((512, 128), F32)],
-        compiler_params=grant(10),
+        compiler_params=grant(6),
         name="turn_edges",
-    )(place, pieces, select)
+    )(pieces, select)
 
 
 def join_and_cut(place, keep, got, edges, got_edges):
@@ -489,7 +502,8 @@
     pieces = lax.all_to_all(pack_edges(act, cot), "tiles", 0, 0, tiled=True)
     keep, send = interior_weights(place, act, cot)
     got = lax.ppermute(send, "tiles", partner)
-    back, edges, send_edges = turn_edges(place, pieces, select)
+    edges, send_edges = edge_weights(place, pieces, select)
+    back = turn_edges(pieces, select)
 
     got_edges = lax.ppermute(send_edges, "tiles", partner)
     quarters = join_and_cut(place, keep, got, edges, got_edges)

time: 98.5 us -> 99.7 us (1.012)
  Pallas kernels: 14.5 us -> 15.5 us
    pallas_call x1 -> x2, Pallas kernels: 1.63 us -> 2.65 us  [the longest x1 1.78 us: edge_weights(): pl.pallas_call(edge_kernel, in_specs=[pl.BlockSpec(memory_space=pltpu.SME...]
where the time goes in v2:
time: 99.7 us; the launch traced here: 99.4 us
  starting transfers between devices  47.5 us (48%)
  waiting for transfers between devices  17.7 us (18%)
  blocking collectives  15.9 us (16%)
  Pallas kernels  15.5 us (16%)
  between operations  1.64 us (2%)
  other arithmetic  1.09 us (1%)
    all_to_all x1, blocking collectives, shards(): lax.all_to_all(copies, 'tiles', 0, 0, tiled=True, axis_index_groups=columns)  15.9 us
    all_to_all x1, starting transfers between devices, shards(): pieces = lax.all_to_all(pack_edges(act, cot), 'tiles', 0, 0, tiled=True)  13 us
    ppermute x4, starting transfers between devices, shards(): theirs.append(lax.ppermute(mine[hop], 'tiles', partner))  12.8 us
    ppermute x6, starting transfers between devices, over_slide(): lax.ppermute(values, 'slide', [(i, (i + hop) % slides) for i in range(sli...  8.33 us
    ppermute x6, starting transfers between devices, over_x(): return lax.ppermute(values, 'tiles', pairs)  8.29 us
    all_to_all x1, waiting for transfers between devices, shards(): pieces = lax.all_to_all(pack_edges(act, cot), 'tiles', 0, 0, tiled=True)  6.12 us
    ppermute x6, waiting for transfers between devices, over_x(): return lax.ppermute(values, 'tiles', pairs)  6.06 us
    ppermute x6, waiting for transfers between devices, over_slide(): lax.ppermute(values, 'slide', [(i, (i + hop) % slides) for i in range(sli...  5.49 us
  transfers between devices with their start and end apart: 20, of which 7 were waited for; matrix products, arithmetic and copies ran while one was open for 1% of the time, Pallas kernels for 11%

profile of v2, /device:TPU:1, one launch (start us, length us, event | category | flops | bytes accessed | tf_op | source)
XLA Modules:
  0.0 99.4 jit_solution(9156513959496136524)
XLA Ops:
  0.7 1.9 %pack_edges.1 = bf16[64,8,128]{2,1,0:T(8,128)(2,1)} custom-call(bf16[64,64,128]{2,1,0:T(8,128)(2,1)} %bitcast.35, bf16[32,32,256]{2,1,0:T(8,128)(2,1)} %bitcast.40), custom_call_target="tpu_custom_call" | custom-call | tf_op jit(solution)/shard_map/pack_edges/pallas_call | solution.py:79
  2.6 13.0 %all-to-all-start = ((bf16[64,8,128]{2,1,0:T(8,128)(2,1)}), bf16[64,8,128]{2,1,0:T(8,128)(2,1)S(1)}, u32[]{:S(2)}, u32[]{:S(2)}) async-start(bf16[64,8,128]{2,1,0:T(8,128)(2,1)} %pack_edges.1), calls=%async_computation | async-start | bytes 262144 | tf_op jit(solution)/shard_map/all_to_all | solution.py:502
  15.6 0.6 fusion.2
  16.8 0.1 stack.27.place_ref
  16.9 2.6 %interior_weights.1 = (f32[1152,128]{1,0:T(8,128)S(1)}, f32[1152,128]{1,0:T(8,128)}) custom-call(s32[5]{0:T(128)S(1)} %stack.27.place_ref, bf16[64,64,128]{2,1,0:T(8,128)(2,1)S(1)} %bitcast.36, bf16[32,32,256]{2,1,0:T(8,128)(2,1)S(1)} %bitcast.41), custom_call_target="tpu_custom_call" | custom-call | flops 603979776 | bytes 3145728 | tf_op jit(solution)/shard_map/interior_weights/pallas_call | solution.py:136
  19.5 0.5 collective-permute-start
  20.0 0.1 fusion
  20.1 0.1 fusion.1
  20.2 0.1 select_dynamic-update-slice_fusion
  20.3 0.1 compare_dynamic-update-slice_fusion
  20.4 0.1 compare_dynamic-update-slice_fusion.1
  20.5 6.1 %all-to-all-done.pieces_ref = bf16[64,8,128]{2,1,0:T(8,128)(2,1)S(1)} async-done(((bf16[64,8,128]{2,1,0:T(8,128)(2,1)}), bf16[64,8,128]{2,1,0:T(8,128)(2,1)S(1)}, u32[]{:S(2)}, u32[]{:S(2)}) %all-to-all-start) | async-done | bytes 131104 | tf_op jit(solution)/shard_map/all_to_all | solution.py:502
  26.7 1.8 %edge_weights.1 = (f32[3,128,128]{2,1,0:T(8,128)S(1)}, f32[3,128,128]{2,1,0:T(8,128)}) custom-call(s32[5]{0:T(128)S(1)} %stack.27.place_ref, bf16[64,8,128]{2,1,0:T(8,128)(2,1)S(1)} %all-to-all-done.pieces_ref, bf16[5,64,64]{2,1,0:T(8,128)(2,1)S(1)} %convert_element_type.10.select_ref), custom_call_target="tpu_custom_call" | custom-call | tf_op jit(solution)/shard_map/edge_weights/pallas_call | solution.py:173
  28.4 0.4 collective-permute-start.1
  28.8 0.9 turn_edges.1
  29.7 4.2 %all-to-all-start.1 = ((bf16[64,8,128]{2,1,0:T(8,128)(2,1)}), bf16[64,8,128]{2,1,0:T(8,128)(2,1)S(1)}, u32[]{:S(2)}, u32[]{:S(2)}) async-start(bf16[64,8,128]{2,1,0:T(8,128)(2,1)} %turn_edges.1), calls=%async_computation.1 | async-start | bytes 262144 | tf_op jit(solution)/shard_map/all_to_all | solution.py:513
  33.9 0.0 collective-permute-done.1.got_edge_ref
  33.9 0.0 collective-permute-done.got_ref
  33.9 0.7 join_and_cut.1
  34.6 0.0 copy-start.1
  34.6 1.4 %collective-permute-start.2 = (f32[288,128]{1,0:T(8,128)S(1)}, f32[288,128]{1,0:T(8,128)S(1)}, u32[]{:S(2)}, u32[]{:S(2)}) collective-permute-start(f32[288,128]{1,0:T(8,128)S(1)} %get-tuple-element.22), channel_id=1, source_target_pairs={{0,1},{1,2},{2,3},{3,0},{4,5},{5,6},{6,7},{7,4},{8,9},{9,10},{10,1... | collective-permute-start | bytes 442376 | tf_op jit(solution)/shard_map/ppermute | solution.py:496
  36.0 2.6 %collective-permute-start.3 = (f32[288,128]{1,0:T(8,128)S(1)}, f32[288,128]{1,0:T(8,128)S(1)}, u32[]{:S(2)}, u32[]{:S(2)}) collective-permute-start(f32[288,128]{1,0:T(8,128)S(1)} %get-tuple-element.23), channel_id=1, source_target_pairs={{0,2},{1,3},{2,0},{3,1},{4,6},{5,7},{6,4},{7,5},{8,10},{9,11},{10,... | collective-permute-start | bytes 442376 | tf_op jit(solution)/shard_map/ppermute | solution.py:496
  38.6 1.1 %collective-permute-start.4 = (f32[288,128]{1,0:T(8,128)S(1)}, f32[288,128]{1,0:T(8,128)S(1)}, u32[]{:S(2)}, u32[]{:S(2)}) collective-permute-start(f32[288,128]{1,0:T(8,128)S(1)} %get-tuple-element.24), channel_id=1, source_target_pairs={{0,3},{1,0},{2,1},{3,2},{4,7},{5,4},{6,5},{7,6},{8,11},{9,8},{10,9... | collective-permute-start | bytes 442376 | tf_op jit(solution)/shard_map/ppermute | solution.py:496
  39.7 1.2 %collective-permute-done.2.refs_1_ = f32[288,128]{1,0:T(8,128)S(1)} collective-permute-done((f32[288,128]{1,0:T(8,128)S(1)}, f32[288,128]{1,0:T(8,128)S(1)}, u32[]{:S(2)}, u32[]{:S(2)}) %collective-permute-start.2) | collective-permute-done | bytes 147488 | tf_op jit(solution)/shard_map/ppermute | solution.py:496
  40.9 4.3 %collective-permute-done.3.refs_2_ = f32[288,128]{1,0:T(8,128)S(1)} collective-permute-done((f32[288,128]{1,0:T(8,128)S(1)}, f32[288,128]{1,0:T(8,128)S(1)}, u32[]{:S(2)}, u32[]{:S(2)}) %collective-permute-start.3) | collective-permute-done | bytes 147488 | tf_op jit(solution)/shard_map/ppermute | solution.py:496
  45.2 0.6 sum_and_cut.1
  45.7 1.6 %collective-permute-start.5 = (f32[72,128]{1,0:T(8,128)S(1)}, f32[72,128]{1,0:T(8,128)S(1)}, u32[]{:S(2)}, u32[]{:S(2)}) collective-permute-start(f32[72,128]{1,0:T(8,128)S(1)} %get-tuple-element.26), channel_id=1, source_target_pairs={{0,8},{4,12},{8,16},{12,20},{16,24},{20,28},{24,0},{28,4},{32,40},... | collective-permute-start | bytes 110600 | tf_op jit(solution)/shard_map/ppermute | solution.py:500
  47.3 2.4 %collective-permute-start.6 = (f32[72,128]{1,0:T(8,128)S(1)}, f32[72,128]{1,0:T(8,128)S(1)}, u32[]{:S(2)}, u32[]{:S(2)}) collective-permute-start(f32[72,128]{1,0:T(8,128)S(1)} %get-tuple-element.27), channel_id=1, source_target_pairs={{0,16},{4,20},{8,24},{12,28},{16,0},{20,4},{24,8},{28,12},{32,48},... | collective-permute-start | bytes 110600 | tf_op jit(solution)/shard_map/ppermute | solution.py:500
  49.7 1.2 %collective-permute-start.7 = (f32[72,128]{1,0:T(8,128)S(1)}, f32[72,128]{1,0:T(8,128)S(1)}, u32[]{:S(2)}, u32[]{:S(2)}) collective-permute-start(f32[72,128]{1,0:T(8,128)S(1)} %get-tuple-element.28), channel_id=1, source_target_pairs={{0,24},{4,28},{8,0},{12,4},{16,8},{20,12},{24,16},{28,20},{32,56},... | collective-permute-start | bytes 110600 | tf_op jit(solution)/shard_map/ppermute | solution.py:500
  50.9 0.0 collective-permute-done.5.refs_1_
  50.9 0.8 collective-permute-done.6.refs_2_
  51.7 1.6 %collective-permute-done.7.refs_3_ = f32[72,128]{1,0:T(8,128)S(1)} collective-permute-done((f32[72,128]{1,0:T(8,128)S(1)}, f32[72,128]{1,0:T(8,128)S(1)}, u32[]{:S(2)}, u32[]{:S(2)}) %collective-permute-start.7) | collective-permute-done | bytes 36896 | tf_op jit(solution)/shard_map/ppermute | solution.py:500
  53.3 15.9 %all_to_all.15.parts_ref = f32[8,72,128]{2,1,0:T(8,128)S(1)} all-to-all(f32[8,72,128]{2,1,0:T(8,128)S(1)} %shard_map.67), channel_id=1, replica_groups={{0,32,64,96,128,160,192,224},{4,36,68,100,132,164,196,228},{8,40,72,104..., dimensions={0} | all-to-all | bytes 589824 | tf_op jit(solution)/shard_map/all_to_all | solution.py:520
  69.2 2.4 %collective-permute-start.10 = (f32[72,128]{1,0:T(8,128)S(1)}, f32[72,128]{1,0:T(8,128)S(1)}, u32[]{:S(2)}, u32[]{:S(2)}) collective-permute-start(f32[72,128]{1,0:T(8,128)S(1)} %sum_scaled.1.refs_0_), channel_id=1, source_target_pairs={{0,24},{4,28},{8,0},{12,4},{16,8},{20,12},{24,16},{28,20},{32,56},... | collective-permute-start | bytes 110600 | tf_op jit(solution)/shard_map/ppermute | solution.py:500
  71.7 0.7 collective-permute-start.8
  72.3 0.4 collective-permute-done.10.refs_3_
  72.7 3.3 %collective-permute-done.9.refs_2_ = f32[72,128]{1,0:T(8,128)S(1)} collective-permute-done((f32[72,128]{1,0:T(8,128)S(1)}, f32[72,128]{1,0:T(8,128)S(1)}, u32[]{:S(2)}, u32[]{:S(2)}) %collective-permute-start.9) | collective-permute-done | bytes 36896 | tf_op jit(solution)/shard_map/ppermute | solution.py:500
  76.1 0.0 collective-permute-done.8.refs_1_
  76.1 0.6 assemble.1.refs_0_
  76.6 2.4 %collective-permute-start.13 = (f32[288,128]{1,0:T(8,128)S(1)}, f32[288,128]{1,0:T(8,128)S(1)}, u32[]{:S(2)}, u32[]{:S(2)}) collective-permute-start(f32[288,128]{1,0:T(8,128)S(1)} %assemble.1.refs_0_), channel_id=1, source_target_pairs={{0,3},{1,0},{2,1},{3,2},{4,7},{5,4},{6,5},{7,6},{8,11},{9,8},{10,9... | collective-permute-start | bytes 442376 | tf_op jit(solution)/shard_map/ppermute | solution.py:496
  79.0 0.9 collective-permute-start.12
  79.9 6.3 %collective-permute-start.14 = (f32[288,128]{1,0:T(8,128)S(1)}, f32[288,128]{1,0:T(8,128)S(1)}, u32[]{:S(2)}, u32[]{:S(2)}) collective-permute-start(f32[288,128]{1,0:T(8,128)S(1)} %assemble.1.refs_0_), channel_id=1, source_target_pairs={{0,4},{4,0},{8,12},{12,8},{16,20},{20,16},{24,28},{28,24},{32,36},... | collective-permute-start | bytes 442376 | tf_op jit(solution)/shard_map/ppermute | solution.py:536
  86.2 2.6 %collective-permute-start.17 = (f32[288,128]{1,0:T(8,128)S(1)}, f32[288,128]{1,0:T(8,128)S(1)}, u32[]{:S(2)}, u32[]{:S(2)}) collective-permute-start(f32[288,128]{1,0:T(8,128)S(1)} %collective-permute-done.13.refs_3_), channel_id=1, source_target_pairs={{0,4},{4,0},{8,12},{12,8},{16,20},{20,16},{24,28},{28,24},{32,36},... | collective-permute-start | bytes 442376 | tf_op jit(solution)/shard_map/ppermute | solution.py:536
  88.8 2.5 %collective-permute-start.16 = (f32[288,128]{1,0:T(8,128)S(1)}, f32[288,128]{1,0:T(8,128)S(1)}, u32[]{:S(2)}, u32[]{:S(2)}) collective-permute-start(f32[288,128]{1,0:T(8,128)S(1)} %collective-permute-done.12.refs_2_), channel_id=1, source_target_pairs={{0,4},{4,0},{8,12},{12,8},{16,20},{20,16},{24,28},{28,24},{32,36},... | collective-permute-start | bytes 442376 | tf_op jit(solution)/shard_map/ppermute | solution.py:536
  91.3 1.5 %collective-permute-start.15 = (f32[288,128]{1,0:T(8,128)S(1)}, f32[288,128]{1,0:T(8,128)S(1)}, u32[]{:S(2)}, u32[]{:S(2)}) collective-permute-start(f32[288,128]{1,0:T(8,128)S(1)} %collective-permute-done.11.refs_1_), channel_id=1, source_target_pairs={{0,4},{4,0},{8,12},{12,8},{16,20},{20,16},{24,28},{28,24},{32,36},... | collective-permute-start | bytes 442376 | tf_op jit(solution)/shard_map/ppermute | solution.py:536
  92.8 2.2 %tile_features.1 = bf16[32,32,256]{2,1,0:T(8,128)(2,1)} custom-call(s32[1]{0:T(128)} %bitcast.live_ref, bf16[64,64,128]{2,1,0:T(8,128)(2,1)S(1)} %bitcast.37, bf16[1152,256]{1,0:T(8,128)(2,1)S(1)} %bitcast.38, bf16[64,8,128]{2,1,0:T(8,128)(2,1)S(1)} %all-to-all-done.1.halo_ref), custom_call_target="tpu_custom_call" | custom-call | flops 603979776 | bytes 2097152 | tf_op jit(solution)/shard_map/tile_features/pallas_call | solution.py:369
  95.0 2.6 %tile_gradient.1 = bf16[64,64,128]{2,1,0:T(8,128)(2,1)} custom-call(s32[1]{0:T(128)} %bitcast.live_ref, bf16[32,32,256]{2,1,0:T(8,128)(2,1)S(1)} %bitcast.42, bf16[1152,256]{1,0:T(8,128)(2,1)S(1)} %bitcast.39, bf16[64,8,128]{2,1,0:T(8,128)(2,1)S(1)} %all-to-all-done.1.halo_ref), custom_call_target="tpu_custom_call" | custom-call | flops 905969664 | bytes 3145728 | tf_op jit(solution)/shard_map/tile_gradient/pallas_call | solution.py:457
  97.7 1.6 %final_weights.1 = f32[1152,256]{1,0:T(8,128)} custom-call(s32[5]{0:T(128)S(1)} %stack.27.place_ref, f32[288,128]{1,0:T(8,128)S(1)} %assemble.1.refs_0_, f32[288,128]{1,0:T(8,128)S(1)} %collective-permute-done.11.refs_1_, f32[288,128]{1,0:T(8,128)S(1)} %collective-permute-done.12.refs_2_, f32[288,128]{1,0:T(8,128)S(1)} %collective-permute-done.13.refs_3_, ...), custom_call_target="tpu_custom_call" | custom-call | tf_op jit(solution)/shard_map/final_weights/pallas_call | solution.py:336
  (23 shorter events, 0.1 us)
Async XLA Ops:
  0.6 16.3 %copy-start.2 = (bf16[1,1,32,32,256]{4,3,2,1,0:T(8,128)(2,1)S(1)}, bf16[1,1,32,32,256]{4,3,2,1,0:T(8,128)(2,1)}, u32[]{:S(2)}) copy-start(bf16[1,1,32,32,256]{4,3,2,1,0:T(8,128)(2,1)} %param.5) | copy-start | bytes 1572868
  0.6 16.3 %copy-start = (bf16[1,1,64,64,128]{4,3,2,1,0:T(8,128)(2,1)S(1)}, bf16[1,1,64,64,128]{4,3,2,1,0:T(8,128)(2,1)}, u32[]{:S(2)}) copy-start(bf16[1,1,64,64,128]{4,3,2,1,0:T(8,128)(2,1)} %param.4) | copy-start | bytes 3145732
  0.7 14.9 %copy-start.3 = (s32[1,64]{1,0:T(1,128)S(1)}, s32[1,64]{1,0:T(1,128)}, u32[]{:S(2)}) copy-start(s32[1,64]{1,0:T(1,128)} %param.7) | copy-start | bytes 772
  2.6 24.1 %all-to-all-start = ((bf16[64,8,128]{2,1,0:T(8,128)(2,1)}), bf16[64,8,128]{2,1,0:T(8,128)(2,1)S(1)}, u32[]{:S(2)}, u32[]{:S(2)}) async-start(bf16[64,8,128]{2,1,0:T(8,128)(2,1)} %pack_edges.1), calls=%async_computation | async-start | bytes 262144 | tf_op jit(solution)/shard_map/all_to_all | solution.py:502
  19.5 14.4 %collective-permute-start = (f32[1152,128]{1,0:T(8,128)}, f32[1152,128]{1,0:T(8,128)S(1)}, u32[]{:S(2)}, u32[]{:S(2)}) collective-permute-start(f32[1152,128]{1,0:T(8,128)} %get-tuple-element.18), channel_id=1, source_target_pairs={{0,4},{4,0},{8,12},{12,8},{16,20},{20,16},{24,28},{28,24},{32,36},... | collective-permute-start | bytes 1769480 | tf_op jit(solution)/shard_map/ppermute | solution.py:504
  28.4 5.5 %collective-permute-start.1 = (f32[3,128,128]{2,1,0:T(8,128)}, f32[3,128,128]{2,1,0:T(8,128)S(1)}, u32[]{:S(2)}, u32[]{:S(2)}) collective-permute-start(f32[3,128,128]{2,1,0:T(8,128)} %get-tuple-element.20), channel_id=1, source_target_pairs={{0,4},{4,0},{8,12},{12,8},{16,20},{20,16},{24,28},{28,24},{32,36},... | collective-permute-start | bytes 589832 | tf_op jit(solution)/shard_map/ppermute | solution.py:508
  29.7 23.6 %all-to-all-start.1 = ((bf16[64,8,128]{2,1,0:T(8,128)(2,1)}), bf16[64,8,128]{2,1,0:T(8,128)(2,1)S(1)}, u32[]{:S(2)}, u32[]{:S(2)}) async-start(bf16[64,8,128]{2,1,0:T(8,128)(2,1)} %turn_edges.1), calls=%async_computation.1 | async-start | bytes 262144 | tf_op jit(solution)/shard_map/all_to_all | solution.py:513
  34.6 58.2 %copy-start.1 = (bf16[3,3,128,256]{3,2,1,0:T(8,128)(2,1)S(1)}, bf16[3,3,128,256]{3,2,1,0:T(8,128)(2,1)}, u32[]{:S(2)}) copy-start(bf16[3,3,128,256]{3,2,1,0:T(8,128)(2,1)} %param.6) | copy-start | bytes 1769476
  34.6 6.3 %collective-permute-start.2 = (f32[288,128]{1,0:T(8,128)S(1)}, f32[288,128]{1,0:T(8,128)S(1)}, u32[]{:S(2)}, u32[]{:S(2)}) collective-permute-start(f32[288,128]{1,0:T(8,128)S(1)} %get-tuple-element.22), channel_id=1, source_target_pairs={{0,1},{1,2},{2,3},{3,0},{4,5},{5,6},{6,7},{7,4},{8,9},{9,10},{10,1... | collective-permute-start | bytes 442376 | tf_op jit(solution)/shard_map/ppermute | solution.py:496
  36.0 9.2 %collective-permute-start.3 = (f32[288,128]{1,0:T(8,128)S(1)}, f32[288,128]{1,0:T(8,128)S(1)}, u32[]{:S(2)}, u32[]{:S(2)}) collective-permute-start(f32[288,128]{1,0:T(8,128)S(1)} %get-tuple-element.23), channel_id=1, source_target_pairs={{0,2},{1,3},{2,0},{3,1},{4,6},{5,7},{6,4},{7,5},{8,10},{9,11},{10,... | collective-permute-start | bytes 442376 | tf_op jit(solution)/shard_map/ppermute | solution.py:496
  38.6 6.6 %collective-permute-start.4 = (f32[288,128]{1,0:T(8,128)S(1)}, f32[288,128]{1,0:T(8,128)S(1)}, u32[]{:S(2)}, u32[]{:S(2)}) collective-permute-start(f32[288,128]{1,0:T(8,128)S(1)} %get-tuple-element.24), channel_id=1, source_target_pairs={{0,3},{1,0},{2,1},{3,2},{4,7},{5,4},{6,5},{7,6},{8,11},{9,8},{10,9... | collective-permute-start | bytes 442376 | tf_op jit(solution)/shard_map/ppermute | solution.py:496
  45.7 5.2 %collective-permute-start.5 = (f32[72,128]{1,0:T(8,128)S(1)}, f32[72,128]{1,0:T(8,128)S(1)}, u32[]{:S(2)}, u32[]{:S(2)}) collective-permute-start(f32[72,128]{1,0:T(8,128)S(1)} %get-tuple-element.26), channel_id=1, source_target_pairs={{0,8},{4,12},{8,16},{12,20},{16,24},{20,28},{24,0},{28,4},{32,40},... | collective-permute-start | bytes 110600 | tf_op jit(solution)/shard_map/ppermute | solution.py:500
  47.3 4.3 %collective-permute-start.6 = (f32[72,128]{1,0:T(8,128)S(1)}, f32[72,128]{1,0:T(8,128)S(1)}, u32[]{:S(2)}, u32[]{:S(2)}) collective-permute-start(f32[72,128]{1,0:T(8,128)S(1)} %get-tuple-element.27), channel_id=1, source_target_pairs={{0,16},{4,20},{8,24},{12,28},{16,0},{20,4},{24,8},{28,12},{32,48},... | collective-permute-start | bytes 110600 | tf_op jit(solution)/shard_map/ppermute | solution.py:500
  49.7 3.5 %collective-permute-start.7 = (f32[72,128]{1,0:T(8,128)S(1)}, f32[72,128]{1,0:T(8,128)S(1)}, u32[]{:S(2)}, u32[]{:S(2)}) collective-permute-start(f32[72,128]{1,0:T(8,128)S(1)} %get-tuple-element.28), channel_id=1, source_target_pairs={{0,24},{4,28},{8,0},{12,4},{16,8},{20,12},{24,16},{28,20},{32,56},... | collective-permute-start | bytes 110600 | tf_op jit(solution)/shard_map/ppermute | solution.py:500
  69.2 3.5 %collective-permute-start.10 = (f32[72,128]{1,0:T(8,128)S(1)}, f32[72,128]{1,0:T(8,128)S(1)}, u32[]{:S(2)}, u32[]{:S(2)}) collective-permute-start(f32[72,128]{1,0:T(8,128)S(1)} %sum_scaled.1.refs_0_), channel_id=1, source_target_pairs={{0,24},{4,28},{8,0},{12,4},{16,8},{20,12},{24,16},{28,20},{32,56},... | collective-permute-start | bytes 110600 | tf_op jit(solution)/shard_map/ppermute | solution.py:500
  71.7 4.4 %collective-permute-start.9 = (f32[72,128]{1,0:T(8,128)S(1)}, f32[72,128]{1,0:T(8,128)S(1)}, u32[]{:S(2)}, u32[]{:S(2)}) collective-permute-start(f32[72,128]{1,0:T(8,128)S(1)} %sum_scaled.1.refs_0_), channel_id=1, source_target_pairs={{0,16},{4,20},{8,24},{12,28},{16,0},{20,4},{24,8},{28,12},{32,48},... | collective-permute-start | bytes 110600 | tf_op jit(solution)/shard_map/ppermute | solution.py:500
  71.7 4.4 %collective-permute-start.8 = (f32[72,128]{1,0:T(8,128)S(1)}, f32[72,128]{1,0:T(8,128)S(1)}, u32[]{:S(2)}, u32[]{:S(2)}) collective-permute-start(f32[72,128]{1,0:T(8,128)S(1)} %sum_scaled.1.refs_0_), channel_id=1, source_target_pairs={{0,8},{4,12},{8,16},{12,20},{16,24},{20,28},{24,0},{28,4},{32,40},... | collective-permute-start | bytes 110600 | tf_op jit(solution)/shard_map/ppermute | solution.py:500
  76.6 9.6 %collective-permute-start.13 = (f32[288,128]{1,0:T(8,128)S(1)}, f32[288,128]{1,0:T(8,128)S(1)}, u32[]{:S(2)}, u32[]{:S(2)}) collective-permute-start(f32[288,128]{1,0:T(8,128)S(1)} %assemble.1.refs_0_), channel_id=1, source_target_pairs={{0,3},{1,0},{2,1},{3,2},{4,7},{5,4},{6,5},{7,6},{8,11},{9,8},{10,9... | collective-permute-start | bytes 442376 | tf_op jit(solution)/shard_map/ppermute | solution.py:496
  79.0 9.8 %collective-permute-start.12 = (f32[288,128]{1,0:T(8,128)S(1)}, f32[288,128]{1,0:T(8,128)S(1)}, u32[]{:S(2)}, u32[]{:S(2)}) collective-permute-start(f32[288,128]{1,0:T(8,128)S(1)} %assemble.1.refs_0_), channel_id=1, source_target_pairs={{0,2},{1,3},{2,0},{3,1},{4,6},{5,7},{6,4},{7,5},{8,10},{9,11},{10,... | collective-permute-start | bytes 442376 | tf_op jit(solution)/shard_map/ppermute | solution.py:496
  79.9 11.4 %collective-permute-start.11 = (f32[288,128]{1,0:T(8,128)S(1)}, f32[288,128]{1,0:T(8,128)S(1)}, u32[]{:S(2)}, u32[]{:S(2)}) collective-permute-start(f32[288,128]{1,0:T(8,128)S(1)} %assemble.1.refs_0_), channel_id=1, source_target_pairs={{0,1},{1,2},{2,3},{3,0},{4,5},{5,6},{6,7},{7,4},{8,9},{9,10},{10,1... | collective-permute-start | bytes 442376 | tf_op jit(solution)/shard_map/ppermute | solution.py:496
  79.9 17.7 %collective-permute-start.14 = (f32[288,128]{1,0:T(8,128)S(1)}, f32[288,128]{1,0:T(8,128)S(1)}, u32[]{:S(2)}, u32[]{:S(2)}) collective-permute-start(f32[288,128]{1,0:T(8,128)S(1)} %assemble.1.refs_0_), channel_id=1, source_target_pairs={{0,4},{4,0},{8,12},{12,8},{16,20},{20,16},{24,28},{28,24},{32,36},... | collective-permute-start | bytes 442376 | tf_op jit(solution)/shard_map/ppermute | solution.py:536
  86.2 11.5 %collective-permute-start.17 = (f32[288,128]{1,0:T(8,128)S(1)}, f32[288,128]{1,0:T(8,128)S(1)}, u32[]{:S(2)}, u32[]{:S(2)}) collective-permute-start(f32[288,128]{1,0:T(8,128)S(1)} %collective-permute-done.13.refs_3_), channel_id=1, source_target_pairs={{0,4},{4,0},{8,12},{12,8},{16,20},{20,16},{24,28},{28,24},{32,36},... | collective-permute-start | bytes 442376 | tf_op jit(solution)/shard_map/ppermute | solution.py:536
  88.8 8.8 %collective-permute-start.16 = (f32[288,128]{1,0:T(8,128)S(1)}, f32[288,128]{1,0:T(8,128)S(1)}, u32[]{:S(2)}, u32[]{:S(2)}) collective-permute-start(f32[288,128]{1,0:T(8,128)S(1)} %collective-permute-done.12.refs_2_), channel_id=1, source_target_pairs={{0,4},{4,0},{8,12},{12,8},{16,20},{20,16},{24,28},{28,24},{32,36},... | collective-permute-start | bytes 442376 | tf_op jit(solution)/shard_map/ppermute | solution.py:536
  91.3 6.4 %collective-permute-start.15 = (f32[288,128]{1,0:T(8,128)S(1)}, f32[288,128]{1,0:T(8,128)S(1)}, u32[]{:S(2)}, u32[]{:S(2)}) collective-permute-start(f32[288,128]{1,0:T(8,128)S(1)} %collective-permute-done.11.refs_1_), channel_id=1, source_target_pairs={{0,4},{4,0},{8,12},{12,8},{16,20},{20,16},{24,28},{28,24},{32,36},... | collective-permute-start | bytes 442376 | tf_op jit(solution)/shard_map/ppermute | solution.py:536
